TPU v7x, 128 devices: a whole 4x4x4 slice. The times are simulated.
128 devices in a mesh: ctx: 32 (over x, z, core), tp: 4 (over y).
Axes of the slice: x: 4, y: 4, z: 4, core: 2. Of those that a mesh axis runs over, the one named last changes fastest.
Arguments:
- residual: bfloat16 [8192, 8192], P('ctx', 'tp'), may hold values from -40 to 40
- query_in: bfloat16 [8192, 8192], P('ctx', 'tp'), may hold values from -6 to 6
- key_in: bfloat16 [8192, 8192], P('ctx', 'tp'), may hold values from -6 to 6
- value_in: bfloat16 [8192, 8192], P('ctx', 'tp'), may hold values from -6 to 6
- short_filter: float32 [3, 7, 8192], P(None, None, 'tp'), may hold values from -2 to 2
- residues: float32 [16, 8192], P(None, 'tp'), may hold values from -0.32 to 0.32
- decay_rate: float32 [16, 8192], P(None, 'tp'), may hold values from 2.4414063e-05 to 0.05
- skip_gain: float32 [8192], P('tp'), may hold values from 0.5 to 1.5
- norm_gain: float32 [8192], P('tp'), may hold values from 0.5 to 1.5
- cotangent: bfloat16 [8192, 8192], P('ctx', 'tp'), may hold values from -6 to 6
Outputs:
- normed: bfloat16 [8192, 8192], P('ctx', 'tp')
- grad_residual: bfloat16 [8192, 8192], P('ctx', 'tp')
- grad_query: bfloat16 [8192, 8192], P('ctx', 'tp')
- grad_key: bfloat16 [8192, 8192], P('ctx', 'tp')
- grad_value: bfloat16 [8192, 8192], P('ctx', 'tp')
- grad_short: float32 [3, 7, 8192], P(None, None, 'tp')
- grad_residues: float32 [16, 8192], P(None, 'tp')
- grad_rate: float32 [16, 8192], P(None, 'tp')
- grad_skip: float32 [8192], P('tp')
- grad_norm_gain: float32 [8192], P('tp')
All inputs are finite; a program needn't handle non-finite values.
Results may differ from a plain program's by a relative error of at most 0.002.
Values may be sent and summed in bfloat16 or wider, within the bound.
A program may use at most 128 MiB of HBM per device.

v0:
```python
import jax
import jax.numpy as jnp
from jax import lax
from jax.sharding import PartitionSpec as P

D = 8192


exact_mode = lax.Precision.HIGHEST


def prefix(value, axis, join, neutral, backward):
    count, mine = (lax.axis_size(axis), lax.axis_index(axis))
    pieces = jax.tree.map(lambda part: lax.all_gather(part, axis), value)
    if backward:
        pieces = jax.tree.map(lambda part: part[::-1], pieces)
        mine = count - 1 - mine
    so_far = jax.tree.map(
        lambda part, zero: jnp.full_like(part, 0) + jnp.asarray(zero, part.dtype), value, neutral
    )

    def lap(position, so_far):
        longer = join(so_far, jax.tree.map(lambda part: part[position], pieces))
        return jax.tree.map(lambda new, old: jnp.where(position < mine, new, old), longer, so_far)

    return lax.fori_loop(0, count - 1, lap, so_far)


def shifted(block, axis, distance):
    devices = range(lax.axis_size(axis))
    route = [(i - distance, i) for i in devices if i - distance in devices]
    return lax.ppermute(block, axis, route)


def as_sent(value):

    def short(part):
        return part.astype(jnp.bfloat16) if part.dtype == jnp.float32 else part

    return jax.tree.map(short, value)


def make_tables(decay_rate, residues, block_len):
    lag_values = jnp.arange(block_len).astype(jnp.float32)
    powers = jnp.exp(-decay_rate[None, :, :] * lag_values[:, None, None])
    kernel = jnp.einsum("kmc,mc->kc", powers, residues, precision=exact_mode)
    offsets = jnp.arange(block_len)
    shifter = (offsets[:, None, None] - offsets[None, :, None] == offsets[None, None, :]).astype(
        jnp.float32
    )
    toeplitz = jnp.einsum("tsk,kc->tsc", shifter, kernel, precision=exact_mode)
    return (lag_values, powers, shifter, toeplitz)


def short_conv(extended, taps, row_count):
    tap_count = taps.shape[0]
    result = taps[0] * extended[tap_count - 1 : tap_count - 1 + row_count]
    for offset in range(1, tap_count):
        result = (
            result
            + taps[offset] * extended[tap_count - 1 - offset : tap_count - 1 - offset + row_count]
        )
    return result


def conv_back(extended_grad, taps, row_count):
    tap_count = taps.shape[0]
    result = taps[0] * extended_grad[0:row_count]
    for offset in range(1, tap_count):
        result = result + taps[offset] * extended_grad[offset : offset + row_count]
    return result


def filter_grad(grad_feat, padded, tap_count, row_count):
    margin = tap_count - 1
    columns = [
        jnp.sum(grad_feat * padded[margin - offset : margin - offset + row_count], axis=0)
        for offset in range(tap_count)
    ]
    return jnp.stack(columns)


def summary_pass(u_blocks, decay_rate, tables):
    lag_values, powers, shifter, toeplitz = tables
    block_len = powers.shape[0]
    behind = powers[::-1]
    behind_lag = behind * lag_values[::-1][:, None, None]
    fading = jnp.exp(-decay_rate * block_len)

    def summary_advance(running, u_block):
        state_x, state_p = running
        gathered = jnp.einsum("smc,sc->mc", behind, u_block, precision=exact_mode)
        weighted = jnp.einsum("smc,sc->mc", behind_lag, u_block, precision=exact_mode)
        state_p = fading * state_p - block_len * fading * state_x - weighted
        state_x = fading * state_x + gathered
        return ((state_x, state_p), None)

    zero_state = jnp.zeros_like(decay_rate)
    (state_x, state_p), _ = lax.scan(summary_advance, (zero_state, zero_state), u_blocks)
    return (state_x, state_p)


def output_pass(u_blocks, state_x, state_p, decay_rate, residues, skip_gain, tables):
    lag_values, powers, shifter, toeplitz = tables
    block_len = powers.shape[0]
    ahead_pow = powers * jnp.exp(-decay_rate)[None]
    behind = powers[::-1]
    fading = jnp.exp(-decay_rate * block_len)

    def output_advance(running, u_block):
        state_x, state_p = running
        inside = jnp.einsum("tsc,sc->tc", toeplitz, u_block, precision=exact_mode)
        carried = jnp.einsum("tmc,mc->tc", ahead_pow, residues * state_x, precision=exact_mode)
        result = inside + carried + skip_gain * u_block
        gathered = jnp.einsum("smc,sc->mc", behind, u_block, precision=exact_mode)
        state_x = fading * state_x + gathered
        return ((state_x, state_p), result)

    (state_x, state_p), results = lax.scan(output_advance, (state_x, state_p), u_blocks)
    return (results, state_x, state_p)


def gradient_pass(u_blocks, dz_blocks, state_x, state_p, decay_rate, tables):
    lag_values, powers, shifter, toeplitz = tables
    block_len = powers.shape[0]
    ahead_pow = powers * jnp.exp(-decay_rate)[None]
    ahead_lag = ahead_pow * (lag_values + 1.0)[:, None, None]
    powers_lag = powers * lag_values[:, None, None]
    behind = powers[::-1]
    behind_lag = behind * lag_values[::-1][:, None, None]
    fading = jnp.exp(-decay_rate * block_len)

    def gradient_advance(running, pair):
        state_x, state_p, sum_res, sum_rate = running
        u_block, dz_block = pair
        products = dz_block[:, None, :] * u_block[None, :, :]
        lagged = jnp.einsum("tsk,tsc->kc", shifter, products, precision=exact_mode)
        nearby = jnp.einsum("tmc,tc->mc", ahead_pow, dz_block, precision=exact_mode)
        nearby_lag = jnp.einsum("tmc,tc->mc", ahead_lag, dz_block, precision=exact_mode)
        sum_res = (
            sum_res
            + jnp.einsum("kc,kmc->mc", lagged, powers, precision=exact_mode)
            + nearby * state_x
        )
        sum_rate = (
            sum_rate
            - jnp.einsum("kc,kmc->mc", lagged, powers_lag, precision=exact_mode)
            - nearby_lag * state_x
            + nearby * state_p
        )
        gathered = jnp.einsum("smc,sc->mc", behind, u_block, precision=exact_mode)
        weighted = jnp.einsum("smc,sc->mc", behind_lag, u_block, precision=exact_mode)
        state_p = fading * state_p - block_len * fading * state_x - weighted
        state_x = fading * state_x + gathered
        return ((state_x, state_p, sum_res, sum_rate), None)

    zero_sum = jnp.zeros_like(state_x)
    (state_x, state_p, sum_res, sum_rate), _ = lax.scan(
        gradient_advance, (state_x, state_p, zero_sum, zero_sum), (u_blocks, dz_blocks)
    )
    return (sum_res, sum_rate)


def adjoint_pass(dz_blocks, adjoint, decay_rate, residues, tables):
    lag_values, powers, shifter, toeplitz = tables
    block_len = powers.shape[0]
    behind_next = powers[::-1] * jnp.exp(-decay_rate)[None]
    fading = jnp.exp(-decay_rate * block_len)

    def adjoint_advance(adjoint, dz_block):
        inside = jnp.einsum("tsc,tc->sc", toeplitz, dz_block, precision=exact_mode)
        carried = jnp.einsum("smc,mc->sc", behind_next, residues * adjoint, precision=exact_mode)
        adjoint = (
            jnp.einsum("tmc,tc->mc", powers, dz_block, precision=exact_mode) + fading * adjoint
        )
        return (adjoint, inside + carried)

    adjoint, results = lax.scan(adjoint_advance, adjoint, dz_blocks, reverse=True)
    return (results, adjoint)


def exit_term(adjoint, decay_rate, residues, lag_values, row_count, block_len):
    starts = jnp.arange(row_count // block_len).astype(jnp.float32) * block_len
    weighted_res = residues * adjoint

    def block_term(start):
        behind_pow = jnp.exp(-decay_rate[None] * (row_count - start - lag_values)[:, None, None])
        return jnp.einsum("smc,mc->sc", behind_pow, weighted_res, precision=exact_mode)

    return lax.map(block_term, starts).reshape(row_count, -1)


def carry_forward(summary, slope_sum, decay_rate, row_count):

    def join_states(earlier, later):
        fading = jnp.exp(-decay_rate * (row_count * later[0]))
        return (
            earlier[0] + later[0],
            fading * earlier[1] + later[1],
            fading * earlier[2] - row_count * later[0] * fading * earlier[1] + later[2],
        )

    neutral = (jnp.zeros((), jnp.float32), jnp.zeros_like(summary), jnp.zeros_like(summary))
    _, state_x, state_p = prefix(
        (jnp.ones((), jnp.float32), summary, slope_sum), "ctx", join_states, neutral, False
    )
    return (state_x, state_p)


def carry_backward(entry_sum, decay_rate, row_count):

    def join_adjoint(earlier, later):
        fading = jnp.exp(-decay_rate * (row_count * later[0]))
        return (earlier[0] + later[0], later[1] + fading * earlier[1])

    neutral = (jnp.zeros((), jnp.float32), jnp.zeros_like(entry_sum))
    _, adjoint = prefix((jnp.ones((), jnp.float32), entry_sum), "ctx", join_adjoint, neutral, True)
    return adjoint


def shards(
    residual,
    query_in,
    key_in,
    value_in,
    short_filter,
    residues,
    decay_rate,
    skip_gain,
    norm_gain,
    cotangent,
):
    row_count = residual.shape[0]
    channels = residual.shape[1]
    tap_count = short_filter.shape[1]
    margin = tap_count - 1
    block_len = min(32, row_count)
    streams = (query_in, key_in, value_in)
    trailing = jnp.stack([stream[row_count - margin :] for stream in streams])
    incoming = shifted(trailing, "ctx", 1)
    padded = [
        jnp.concatenate([incoming[stream_id], streams[stream_id]], axis=0).astype(jnp.float32)
        for stream_id in range(3)
    ]
    featured = [
        short_conv(padded[stream_id], short_filter[stream_id], row_count) for stream_id in range(3)
    ]
    mixed_uv = featured[1] * featured[2]
    tables = make_tables(decay_rate, residues, block_len)
    lag_values = tables[0]
    zero_state = jnp.zeros_like(decay_rate)
    u_blocks = mixed_uv.reshape(row_count // block_len, block_len, channels)
    summary, slope_sum = summary_pass(u_blocks, decay_rate, tables)
    state_x, state_p = carry_forward(summary, slope_sum, decay_rate, row_count)
    modal_blocks, _, _ = output_pass(
        u_blocks, state_x, zero_state, decay_rate, residues, skip_gain, tables
    )
    modal = modal_blocks.reshape(row_count, channels)
    summed = residual.astype(jnp.float32) + featured[0] * modal
    cot_values = cotangent.astype(jnp.float32)
    gain_term = cot_values * norm_gain
    squares, inner_sum = lax.psum(
        (jnp.sum(summed * summed, axis=1), jnp.sum(gain_term * summed, axis=1)), "tp"
    )
    inv_rms = lax.rsqrt(squares / D + 1e-05)
    normed = (summed * inv_rms[:, None] * norm_gain).astype(jnp.bfloat16)
    grad_sum = inv_rms[:, None] * gain_term - summed * (inv_rms**3 * inner_sum / D)[:, None]
    grad_modal = grad_sum * featured[0]
    grad_front = grad_sum * modal
    dz_blocks = grad_modal.reshape(row_count // block_len, block_len, channels)
    sum_res, sum_rate = gradient_pass(u_blocks, dz_blocks, state_x, state_p, decay_rate, tables)
    mixed_blocks, entry_sum = adjoint_pass(dz_blocks, zero_state, decay_rate, residues, tables)
    adjoint = carry_backward(entry_sum, decay_rate, row_count)
    grad_mixed = (
        mixed_blocks.reshape(row_count, channels)
        + exit_term(adjoint, decay_rate, residues, lag_values, row_count, block_len)
        + skip_gain * grad_modal
    )
    grad_feats = (grad_front, grad_mixed * featured[2], grad_mixed * featured[1])
    leading = jnp.stack([grad_feat[:margin] for grad_feat in grad_feats])
    overflow = shifted(as_sent(leading), "ctx", -1).astype(leading.dtype)
    grad_streams = [
        conv_back(
            jnp.concatenate([grad_feats[stream_id], overflow[stream_id]], axis=0),
            short_filter[stream_id],
            row_count,
        ).astype(jnp.bfloat16)
        for stream_id in range(3)
    ]
    local_short = jnp.stack(
        [
            filter_grad(grad_feats[stream_id], padded[stream_id], tap_count, row_count)
            for stream_id in range(3)
        ]
    )
    local_skip = jnp.sum(grad_modal * mixed_uv, axis=0)
    local_gain = jnp.sum(cot_values * summed * inv_rms[:, None], axis=0)
    grad_short, grad_residues, grad_rate, grad_skip, grad_gain = lax.psum(
        (local_short, sum_res, residues * sum_rate, local_skip, local_gain), "ctx"
    )
    return (
        normed,
        grad_sum.astype(jnp.bfloat16),
        grad_streams[0],
        grad_streams[1],
        grad_streams[2],
        grad_short,
        grad_residues,
        grad_rate,
        grad_skip,
        grad_gain,
    )


def solution(mesh):
    placed = (
        P("ctx", "tp"),
        P("ctx", "tp"),
        P("ctx", "tp"),
        P("ctx", "tp"),
        P(None, None, "tp"),
        P(None, "tp"),
        P(None, "tp"),
        P("tp"),
        P("tp"),
        P("ctx", "tp"),
    )
    return jax.shard_map(
        shards,
        mesh=mesh,
        in_specs=placed,
        out_specs=(
            P("ctx", "tp"),
            P("ctx", "tp"),
            P("ctx", "tp"),
            P("ctx", "tp"),
            P("ctx", "tp"),
            P(None, None, "tp"),
            P(None, "tp"),
            P(None, "tp"),
            P("tp"),
            P("tp"),
        ),
        check_vma=False,
    )
```

profile of v0, /device:TPU:1, one launch (start us, length us, event | category | flops | bytes accessed | tf_op | source)
XLA Modules:
  0.0 953.9 jit_solution(4242341893905046392)
XLA Ops:
  8.8 4.9 collective-permute-start
  18.3 4.5 broadcast_multiply_fusion
  23.8 4.6 rev.16
  31.7 4.9 fusion.110
  36.5 44.9 %while.111 = (s32[]{:T(128)}, f32[16,2048]{1,0:T(8,128)S(1)}, f32[16,2048]{1,0:T(8,128)S(1)}, f32[16,2048]{1,0:T(8,128)S(1)}, f32[8,32,2048]{2,1,0:T(8,128)}, /*...) while((s32[]{:T(128)}, f32[16,2048]{1,0:T(8,128)S(1)}, ...), condition=%wide.region_1.2_spmd.clone, body=%wide.region_0.1_spmd.clone.sunk | while | flops 4423683 | bytes 10354795 | solution.py:99
  84.4 62.2 %all-reduce = f32[32]{0:T(128)S(1)} all-reduce(f32[32]{0:T(128)S(1)} %dynamic-update-slice), channel_id=1, replica_groups=mesh['ctx'=32,'tp'=4] {'ctx'}, use_global_device_ids=true, to_apply=%add | all-reduce | flops 32 | bytes 256
  149.6 5.7 fusion.96
  156.9 22.2 %all-gather.9.cloned.1.call-done = f32[512,2048]{1,0:T(8,128)} async-done(((f32[16,2048]{1,0:T(8,128)}), f32[512,2048]{1,0:T(8,128)}) %all-gather.9.cloned.1.call-update) | async-done | bytes 4194320 | tf_op jit(solution)/shard_map/all_gather | solution.py:14
  179.1 72.0 %while.112 = (s32[]{:T(128)}, f32[16,2048]{1,0:T(8,128)S(1)}, f32[16,2048]{1,0:T(8,128)S(1)}, s32[]{:T(128)}, f32[32]{0:T(128)S(1)}, /*index=5*/f32[16,2048]{1,0...) while((s32[]{:T(128)}, f32[16,2048]{1,0:T(8,128)S(1)}, ...), condition=%wide.region_3.4_spmd.clone, body=%wide.region_2.3_spmd.clone.sunk | while | flops 393221 | bytes 917665 | solution.py:26
  253.3 104.5 %while.109 = (s32[]{:T(128)}, f32[16,2048]{1,0:T(8,128)}, f32[8,32,2048]{2,1,0:T(8,128)}, f32[16,2048]{1,0:T(8,128)S(1)}, f32[8,32,2048]{2,1,0:T(8,128)}, /*inde...) while((s32[]{:T(128)}, f32[16,2048]{1,0:T(8,128)}, ...), condition=%wide.region_5.6_spmd.clone, body=%wide.region_4.5_spmd.clone.sunk | while | flops 10616834 | bytes 17048348 | solution.py:119
  259.9 4.8 multiply_reduce_fusion.50
  272.9 4.8 multiply_reduce_fusion.50
  286.0 4.8 multiply_reduce_fusion.50
  299.0 4.8 multiply_reduce_fusion.50
  312.1 4.8 multiply_reduce_fusion.50
  325.2 4.8 multiply_reduce_fusion.50
  338.2 4.8 multiply_reduce_fusion.50
  351.3 4.8 multiply_reduce_fusion.50
  357.8 10.4 %multiply_reduce_fusion.38 = (f32[256]{0:T(256)S(1)}, f32[256,2048]{1,0:T(8,128)}, f32[256,2048]{1,0:T(8,128)}) fusion(f32[8,32,2048]{2,1,0:T(8,128)} %get-tuple-element.774, bf16[256,2048]{1,0:T(8,128)(2,1)} %param.24, f32[262,2048]{1,0:T(8,128)} %maximum_convert_fusion, f32[2048]{0:T(1024)S(1)} %bitcast.320, f32[2048]{0:T(1024)S(1)} %bitcast.322, ...), kind=kLoop, calls=%fused_computation.189 | loop fusion | flops 9436928 | bytes 22078464 | tf_op jit(solution)/shard_map/reduce_sum | solution.py:263
  368.2 8.5 psum.49
  379.1 6.2 psum.50
  385.4 13.9 %multiply_reduce_fusion.31 = (f32[2048]{0:T(1024)S(1)}, f32[2048]{0:T(1024)S(1)}, f32[2048]{0:T(1024)S(1)}, f32[2048]{0:T(1024)S(1)}, f32[2048]{0:T(1024)S(1)}, ...) fusion(f32[262,2048]{1,0:T(8,128)} %maximum_convert_fusion, ...), kind=kLoop, calls=%fused_computation.181 | loop fusion | flops 14139392 | bytes 30484480 | tf_op jit(solution)/shard_map/reduce_sum | solution.py:77
  401.0 99.0 %while.113 = (s32[]{:T(128)}, f32[16,2048]{1,0:T(8,128)}, f32[8,32,2048]{2,1,0:T(8,128)}, f32[8,32,2048]{2,1,0:T(8,128)}, f32[16,2048]{1,0:T(8,128)S(1)}, /*inde...) while((s32[]{:T(128)}, f32[16,2048]{1,0:T(8,128)}, ...), condition=%wide.region_11.12_spmd.clone, body=%wide.region_10.11_spmd.clone.sunk | while | flops 9469956 | bytes 16122139 | solution.py:178
  408.0 4.5 multiply_reduce_fusion.55
  420.4 4.5 multiply_reduce_fusion.55
  432.7 4.5 multiply_reduce_fusion.55
  445.1 4.5 multiply_reduce_fusion.55
  457.5 4.5 multiply_reduce_fusion.55
  469.9 4.5 multiply_reduce_fusion.55
  482.3 4.5 multiply_reduce_fusion.55
  494.6 4.5 multiply_reduce_fusion.55
  501.4 122.4 %all-reduce.1 = (f32[2048]{0:T(1024)}, f32[2048]{0:T(1024)}) all-reduce(f32[2048]{0:T(1024)S(1)} %get-tuple-element.1303, f32[2048]{0:T(1024)S(1)} %get-tuple-element.1130), channel_id=1, replica_groups=mesh['ctx'=32,'tp'=4] {'ctx'}, use_global_device_ids=true, to_apply=%region_43.44 | all-reduce | flops 4096 | bytes 32768 | tf_op jit(solution)/shard_map/psum | solution.py:298
  623.9 96.1 %while.115 = (s32[]{:T(128)}, f32[16,2048]{1,0:T(8,128)S(1)}, f32[16,2048]{1,0:T(8,128)S(1)}, f32[16,2048]{1,0:T(8,128)S(1)}, f32[16,2048]{1,0:T(8,128)S(1)}, /*...) while((s32[]{:T(128)}, f32[16,2048]{1,0:T(8,128)S(1)}, ...), condition=%wide.region_39.40_spmd.clone.clone.clone, body=%wide.region_38.39_spmd.clone.clone.clone.sunk | while | flops 824606720 | bytes 48632316 | solution.py:158
  625.1 5.6 fusion.124
  637.1 5.6 fusion.124
  649.1 5.6 fusion.124
  661.2 5.6 fusion.124
  673.2 5.6 fusion.124
  685.2 5.6 fusion.124
  697.2 5.6 fusion.124
  709.2 5.6 fusion.124
  720.1 4.7 rev.18
  724.8 69.0 %while.114 = (s32[]{:T(128)}, f32[16,2048]{1,0:T(8,128)S(1)}, s32[]{:T(128)}, f32[32,16,2048]{2,1,0:T(8,128)}, f32[32]{0:T(128)S(1)}, /*index=5*/f32[16,2048]{1,0:T(8,128)S(1)}, s32[]{:T(128)}, f32[1]{0:T(128)}, s32[]{:T(128)}) while((s32[]{:T(128)}, f32[16,2048]{1,0:T(8,128)S(1)}, s32[]{:T(128)}, f32[32,16,2048]{2,1,0:T(8,128)}, ...), condition=%wide.region_13.14_spmd.clone, body=%wide.region_12.13_spmd.clone.sunk | while | flops 163845 | bytes 524433 | solution.py:26
  796.1 25.4 %while.110 = (s32[]{:T(128)}, f32[8,32,2048]{2,1,0:T(8,128)}, f32[1,16,2048]{2,1,0:T(8,128)S(1)}, f32[8]{0:T(128)S(1)}, f32[16,2048]{1,0:T(8,128)S(1)}, /*index=5*/s32[]{:T(128)}, f32[1]{0:T(128)}) while((s32[]{:T(128)}, f32[8,32,2048]{2,1,0:T(8,128)}, f32[1,16,2048]{2,1,0:T(8,128)S(1)}, f32[8]{0:T(128)S(1)}, ...), condition=%wide.region_15.16_spmd.clone, body=%wide.region_14.15_spmd.clone.sunk | while | flops 3080259 | bytes 1049449 | solution.py:190
  824.9 6.5 multiply_reduce_fusion.24
  833.4 7.6 collective-permute-start.1
  843.6 8.2 fusion.43
  858.0 84.2 %all-reduce.5.cloned.1.call-done = (f32[3,7,2048]{2,1,0:T(8,128)}, f32[16,2048]{1,0:T(8,128)}, f32[16,2048]{1,0:T(8,128)}) async-done(((f32[3,7,2048]{2,1,0:T(8,128)}, f32[16,2048]{1,0:T(8,128)}, f32[16,2048]{1,0:T(8,128)}), (f32[3,7,2048]{2,1,0:T(8,128)}, f32[16,2048]{1,0:T(8,128)}, f32[16,2048]{1,0:T(8,128)})) %all-reduce.5.cloned.1.call-update) | async-done | bytes 434192 | tf_op jit(solution)/shard_map/psum | solution.py:298
  (544 shorter events, 389.7 us)
Async XLA Ops:
  7.2 149.7 %all-gather.7.cloned.1.call-start = ((), (), s32[]{:S(2)}) async-start(), calls=%async_computation | async-start | bytes 4325376 | tf_op jit(solution)/shard_map/all_gather | solution.py:14
  8.8 19.6 %collective-permute-start = (bf16[3,6,2048]{2,1,0:T(8,128)(2,1)S(1)}, bf16[3,6,2048]{2,1,0:T(8,128)(2,1)S(1)}, u32[]{:S(2)}, u32[]{:S(2)}) collective-permute-start(bf16[3,6,2048]{2,1,0:T(8,128)(2,1)S(1)} %pad_maximum_fusion.4), channel_id=1, source_target_pairs={{0,4},{4,8},{8,12},{12,16},{16,20},{20,24},{24,28},{28,32},{32,36}... | collective-permute-start | bytes 221192 | tf_op jit(solution)/shard_map/ppermute | solution.py:32
  15.5 16.0 %copy-start.30 = (f32[1,1,2048]{2,1,0:T(1,128)}, f32[1,1,2048]{2,1,0:T(1,128)S(1)}, u32[]{:S(2)}) copy-start(f32[1,1,2048]{2,1,0:T(1,128)S(1)} %get-tuple-element.1315) | copy-start | bytes 24580
  15.5 16.0 %copy-start.32 = (f32[1,1,2048]{2,1,0:T(1,128)}, f32[1,1,2048]{2,1,0:T(1,128)S(1)}, u32[]{:S(2)}) copy-start(f32[1,1,2048]{2,1,0:T(1,128)S(1)} %get-tuple-element.1316) | copy-start | bytes 24580
  15.5 16.0 %copy-start.34 = (f32[1,1,2048]{2,1,0:T(1,128)}, f32[1,1,2048]{2,1,0:T(1,128)S(1)}, u32[]{:S(2)}) copy-start(f32[1,1,2048]{2,1,0:T(1,128)S(1)} %get-tuple-element.1317) | copy-start | bytes 24580
  15.5 16.0 %copy-start.36 = (f32[1,1,2048]{2,1,0:T(1,128)}, f32[1,1,2048]{2,1,0:T(1,128)S(1)}, u32[]{:S(2)}) copy-start(f32[1,1,2048]{2,1,0:T(1,128)S(1)} %get-tuple-element.1318) | copy-start | bytes 24580
  15.5 16.0 %copy-start.38 = (f32[1,1,2048]{2,1,0:T(1,128)}, f32[1,1,2048]{2,1,0:T(1,128)S(1)}, u32[]{:S(2)}) copy-start(f32[1,1,2048]{2,1,0:T(1,128)S(1)} %get-tuple-element.1319) | copy-start | bytes 24580
  15.5 16.0 %copy-start.40 = (f32[1,1,2048]{2,1,0:T(1,128)}, f32[1,1,2048]{2,1,0:T(1,128)S(1)}, u32[]{:S(2)}) copy-start(f32[1,1,2048]{2,1,0:T(1,128)S(1)} %get-tuple-element.1320) | copy-start | bytes 24580
  15.5 16.0 %copy-start.42 = (f32[1,1,2048]{2,1,0:T(1,128)}, f32[1,1,2048]{2,1,0:T(1,128)S(1)}, u32[]{:S(2)}) copy-start(f32[1,1,2048]{2,1,0:T(1,128)S(1)} %get-tuple-element.1321) | copy-start | bytes 24580
  15.5 16.0 %copy-start.44 = (f32[1,1,2048]{2,1,0:T(1,128)}, f32[1,1,2048]{2,1,0:T(1,128)S(1)}, u32[]{:S(2)}) copy-start(f32[1,1,2048]{2,1,0:T(1,128)S(1)} %get-tuple-element.1310) | copy-start | bytes 24580
  15.6 16.0 %copy-start.46 = (f32[1,1,2048]{2,1,0:T(1,128)}, f32[1,1,2048]{2,1,0:T(1,128)S(1)}, u32[]{:S(2)}) copy-start(f32[1,1,2048]{2,1,0:T(1,128)S(1)} %get-tuple-element.1311) | copy-start | bytes 24580
  15.6 16.0 %copy-start.48 = (f32[1,1,2048]{2,1,0:T(1,128)}, f32[1,1,2048]{2,1,0:T(1,128)S(1)}, u32[]{:S(2)}) copy-start(f32[1,1,2048]{2,1,0:T(1,128)S(1)} %get-tuple-element.1312) | copy-start | bytes 24580
  15.6 16.0 %copy-start.50 = (f32[1,1,2048]{2,1,0:T(1,128)}, f32[1,1,2048]{2,1,0:T(1,128)S(1)}, u32[]{:S(2)}) copy-start(f32[1,1,2048]{2,1,0:T(1,128)S(1)} %get-tuple-element.1313) | copy-start | bytes 24580
  15.6 16.0 %copy-start.52 = (f32[1,1,2048]{2,1,0:T(1,128)}, f32[1,1,2048]{2,1,0:T(1,128)S(1)}, u32[]{:S(2)}) copy-start(f32[1,1,2048]{2,1,0:T(1,128)S(1)} %get-tuple-element.1314) | copy-start | bytes 24580
  15.6 342.2 %copy-start.22 = (f32[1,1,2048]{2,1,0:T(1,128)}, f32[1,1,2048]{2,1,0:T(1,128)S(1)}, u32[]{:S(2)}) copy-start(f32[1,1,2048]{2,1,0:T(1,128)S(1)} %get-tuple-element.1324) | copy-start | bytes 24580
  15.6 342.2 %copy-start.24 = (f32[1,1,2048]{2,1,0:T(1,128)}, f32[1,1,2048]{2,1,0:T(1,128)S(1)}, u32[]{:S(2)}) copy-start(f32[1,1,2048]{2,1,0:T(1,128)S(1)} %get-tuple-element.1325) | copy-start | bytes 24580
  15.6 342.2 %copy-start.26 = (f32[1,1,2048]{2,1,0:T(1,128)}, f32[1,1,2048]{2,1,0:T(1,128)S(1)}, u32[]{:S(2)}) copy-start(f32[1,1,2048]{2,1,0:T(1,128)S(1)} %get-tuple-element.1326) | copy-start | bytes 24580
  15.6 342.2 %copy-start.28 = (f32[1,1,2048]{2,1,0:T(1,128)}, f32[1,1,2048]{2,1,0:T(1,128)S(1)}, u32[]{:S(2)}) copy-start(f32[1,1,2048]{2,1,0:T(1,128)S(1)} %get-tuple-element.1327) | copy-start | bytes 24580
  36.5 46.5 %copy-start.63 = (u32[128]{0:T(128)S(1)}, u32[128]{0:T(128)}, u32[]{:S(2)}) copy-start(u32[128]{0:T(128)} %constant.186) | copy-start | bytes 1540
  36.5 111.9 %copy-start.6 = (f32[16,2048]{1,0:T(8,128)S(1)}, f32[16,2048]{1,0:T(8,128)}, u32[]{:S(2)}) copy-start(f32[16,2048]{1,0:T(8,128)} %param.29) | copy-start | bytes 393220
  82.1 97.0 %all-gather.9.cloned.1.call-start = ((), (), s32[]{:S(2)}) async-start(), calls=%async_computation.1 | async-start | bytes 4325376 | tf_op jit(solution)/shard_map/all_gather | solution.py:14
  82.9 637.2 %all-gather.11.cloned.1.call-start = ((), (), s32[]{:S(2)}) async-start(), calls=%async_computation.2 | async-start | bytes 4325376 | tf_op jit(solution)/shard_map/all_gather | solution.py:14
  357.8 10.4 %copy-start.59 = (f32[32]{0:T(128)}, f32[32]{0:T(128)S(1)}, u32[]{:S(2)}) copy-start(f32[32]{0:T(128)S(1)} %get-tuple-element.2070) | copy-start | bytes 388
  357.8 18.8 %copy-start.58 = (f32[2048]{0:T(1024)S(1)}, f32[2048]{0:T(1024)}, u32[]{:S(2)}) copy-start(f32[2048]{0:T(1024)} %param.32) | copy-start | bytes 24580
  401.0 222.9 %copy-start.64 = (f32[32]{0:T(128)S(1)}, f32[32]{0:T(128)}, u32[]{:S(2)}) copy-start(f32[32]{0:T(128)} %broadcast_add_fusion) | copy-start | bytes 388
  499.9 442.3 %all-reduce.5.cloned.1.call-start = ((), (), s32[]{:S(2)}) async-start(), calls=%async_computation.3 | async-start | bytes 917504 | tf_op jit(solution)/shard_map/psum | solution.py:298
  625.1 8.6 copy-start
  625.1 8.6 copy-start.1
  637.1 8.6 copy-start
  637.1 8.5 copy-start.1
  649.1 8.6 copy-start
  649.1 8.5 copy-start.1
  661.1 8.6 copy-start
  661.1 8.5 copy-start.1
  673.1 8.6 copy-start
  685.1 8.6 copy-start
  697.2 8.6 copy-start
  709.2 8.6 copy-start
  724.8 71.3 %copy-start.20 = (f32[1,16,2048]{2,1,0:T(8,128)S(1)}, f32[1,16,2048]{2,1,0:T(8,128)}, u32[]{:S(2)}) copy-start(f32[1,16,2048]{2,1,0:T(8,128)} %get-tuple-element.1992) | copy-start | bytes 393220
  724.8 71.3 %copy-start.61 = (f32[8]{0:T(128)S(1)}, f32[8]{0:T(128)}, u32[]{:S(2)}) copy-start(f32[8]{0:T(128)} %convert_multiply_fusion.2) | copy-start | bytes 100
  831.4 12.1 %copy-start.45 = (f32[1,1,2048]{2,1,0:T(1,128)S(1)}, f32[1,1,2048]{2,1,0:T(1,128)}, u32[]{:S(2)}) copy-start(f32[1,1,2048]{2,1,0:T(1,128)} %copy-done.44) | copy-start | bytes 24580
  831.5 12.1 %copy-start.47 = (f32[1,1,2048]{2,1,0:T(1,128)S(1)}, f32[1,1,2048]{2,1,0:T(1,128)}, u32[]{:S(2)}) copy-start(f32[1,1,2048]{2,1,0:T(1,128)} %copy-done.46) | copy-start | bytes 24580
  831.5 12.1 %copy-start.49 = (f32[1,1,2048]{2,1,0:T(1,128)S(1)}, f32[1,1,2048]{2,1,0:T(1,128)}, u32[]{:S(2)}) copy-start(f32[1,1,2048]{2,1,0:T(1,128)} %copy-done.48) | copy-start | bytes 24580
  831.5 12.1 %copy-start.51 = (f32[1,1,2048]{2,1,0:T(1,128)S(1)}, f32[1,1,2048]{2,1,0:T(1,128)}, u32[]{:S(2)}) copy-start(f32[1,1,2048]{2,1,0:T(1,128)} %copy-done.50) | copy-start | bytes 24580
  831.5 12.1 %copy-start.53 = (f32[1,1,2048]{2,1,0:T(1,128)S(1)}, f32[1,1,2048]{2,1,0:T(1,128)}, u32[]{:S(2)}) copy-start(f32[1,1,2048]{2,1,0:T(1,128)} %copy-done.52) | copy-start | bytes 24580
  831.5 12.1 %copy-start.55 = (f32[1,1,2048]{2,1,0:T(1,128)S(1)}, f32[1,1,2048]{2,1,0:T(1,128)}, u32[]{:S(2)}) copy-start(f32[1,1,2048]{2,1,0:T(1,128)} %copy-done.54) | copy-start | bytes 24580
  831.5 12.1 %copy-start.57 = (f32[1,1,2048]{2,1,0:T(1,128)S(1)}, f32[1,1,2048]{2,1,0:T(1,128)}, u32[]{:S(2)}) copy-start(f32[1,1,2048]{2,1,0:T(1,128)} %copy-done.56) | copy-start | bytes 24580
  833.4 10.1 %collective-permute-start.1 = (bf16[3,6,2048]{2,1,0:T(8,128)(2,1)S(1)}, bf16[3,6,2048]{2,1,0:T(8,128)(2,1)S(1)}, u32[]{:S(2)}, u32[]{:S(2)}) collective-permute-start(bf16[3,6,2048]{2,1,0:T(8,128)(2,1)S(1)} %pad_maximum_fusion.5), channel_id=1, source_target_pairs={{4,0},{8,4},{12,8},{16,12},{20,16},{24,20},{28,24},{32,28},{36,32}... | collective-permute-start | bytes 221192 | tf_op jit(solution)/shard_map/ppermute | solution.py:32
  (51 other events, 275.6 us)
Sparse Core Ops, SparseCore 0:
  82.2 48.0 all-gather.6
  133.1 45.9 all-gather.8
  500.1 48.6 all-gather.10
  843.6 98.5 all-reduce.4
where the time goes:
time: 969 us; the launch traced here: 954 us
  other arithmetic  409 us (42%)
  blocking collectives  199 us (21%)
  local copies, waits for them, and re-layouts  112 us (12%)
  waiting for transfers between devices  107 us (11%)
  matrix products  50.2 us (5%)
  loops' own time  48.4 us (5%)
  between operations  15.1 us (2%)
  starting transfers between devices  12.7 us (1%)
    psum x1, blocking collectives, shards(): lax.psum((local_short, sum_res, residues * sum_rate, local_skip, local_ga...  122 us
    psum x1, waiting for transfers between devices, shards(): lax.psum((local_short, sum_res, residues * sum_rate, local_skip, local_ga...  84.2 us
    select_n x62, other arithmetic, lap(): jnp.where(position < mine, new, old)  62.8 us
    unnamed x1, blocking collectives  62.2 us
    dot_general x8, matrix products, gradient_advance(): lagged = jnp.einsum('tsk,tsc->kc', shifter, products, precision=exact_mode)  44.6 us
    another operation x2, loops' own time, prefix(): return lax.fori_loop(0, count - 1, lap, so_far)  41.9 us
    dot_general x8, other arithmetic, output_advance(): inside = jnp.einsum('tsc,sc->tc', toeplitz, u_block, precision=exact_mode)  38.3 us
    dynamic_slice x62, local copies, waits for them, and re-layouts, lap(): longer = join(so_far, jax.tree.map(lambda part: part[position], pieces))  36.3 us
  transfers between devices with their start and end apart: 6, of which 2 were waited for; matrix products, arithmetic and copies ran while one was open for 15% of the time, Pallas kernels for 0%

commit v1 on v0

v1 whole, which is shorter than its diff:
```python
import functools

import jax
import jax.numpy as jnp
from jax import lax
from jax.experimental import pallas as pl
from jax.experimental.pallas import tpu as pltpu
from jax.sharding import PartitionSpec as P

f32 = jnp.float32
bf16 = jnp.bfloat16
MESH = pl.DeviceIdType.MESH
B = 16
M = 16
KS = 7
HALO = KS - 1


def loop(count, step, start=0):
    def lap(i, carry):
        step(i)
        return carry

    lax.fori_loop(start, count, lap, 0)


def total(terms):
    terms = list(terms)
    while len(terms) > 1:
        terms = [
            terms[i] + terms[i + 1] if i + 1 < len(terms) else terms[i]
            for i in range(0, len(terms), 2)
        ]
    return terms[0]


def kernel(
    n, ntp, rows, width,
    res_h, q_h, k_h, v_h, sf_h, r_h, lam_h, skip_h, gain_h, cot_h,
    normed_o, gres_o, gq_o, gk_o, gv_o, short_o, gr_o, gl_o, gskip_o, ggain_o,
    nat, halo, sfv, rv, lv, skipv, gainv,
    QX, KX, VX, RS, CT, F0, F1, F2, U, Y, DZ, GS, G, GF0, GF1, GF2,
    AP, WP, KT, RT, SW, AT, XB, PB, AB,
    S1, R1, E1, X0, S2, R2, E2, A0,
    sums, tpr, INVT, CFT, RA, SA, CK, SG,
    T1, RR1, SUM1, AG1, T2, RR2, SUM2, AG2,
    shv, grv, glv,
    insem, outsem, ssem, rsem, hssem, hrsem,
):
    H = width // 1024
    nb = rows // B
    D = width * ntp
    me = lax.axis_index("ctx")
    mt = lax.axis_index("tp")
    tiles = H * M
    k1 = tiles // n
    k2 = 64 // n

    def peer(p):
        return (p, mt)

    ins = [
        (k_h, nat.at[2]), (v_h, nat.at[3]), (q_h, nat.at[1]), (res_h, nat.at[0]), (cot_h, nat.at[4]),
        (sf_h, sfv), (r_h, rv), (lam_h, lv), (skip_h, skipv), (gain_h, gainv),
    ]
    in_copies = [pltpu.make_async_copy(s, d, insem.at[i]) for i, (s, d) in enumerate(ins)]
    for copy in in_copies:
        copy.start()

    barrier = pltpu.get_barrier_semaphore()

    def greet(i):
        pl.semaphore_signal(
            barrier, inc=1, device_id=peer(lax.rem(me + i, n)), device_id_type=MESH
        )

    loop(n, greet, 1)
    for i in range(1, ntp):
        pl.semaphore_signal(
            barrier, inc=1, device_id=(me, lax.rem(mt + i, ntp)), device_id_type=MESH
        )
    pl.semaphore_wait(barrier, n - 1 + ntp - 1)

    def in_halo(i, src):
        return pltpu.make_async_remote_copy(
            src_ref=src.at[pl.ds(rows - 16, 16)], dst_ref=halo.at[i],
            send_sem=hssem.at[i], recv_sem=hrsem.at[i],
            device_id=peer(lax.rem(me + 1, n)), device_id_type=MESH,
        )

    halo_copies = [in_halo(0, q_h), in_halo(1, k_h), in_halo(2, v_h)]

    @pl.when(me < n - 1)
    def _():
        for copy in halo_copies:
            copy.start()

    for i in range(5, 10):
        in_copies[i].wait()
    for h in range(H):
        cols = pl.ds(h * 1024, 1024)
        lam = lv[:, cols].reshape(M, 8, 128)
        r = rv[:, cols].reshape(M, 8, 128)
        RT[h] = r
        AT[pl.ds(h * M, M)] = jnp.exp(lam * (-float(rows)))
        for i in range(3):
            SG[0:8, :] = jnp.zeros((8, 1024), f32)
            SG[0:KS, :] = sfv[i, :, cols]
            SW[i, h] = SG[0:8, :].reshape(8, 8, 128)

        def powers(k):
            p = jnp.exp(lam * (-k.astype(f32)))
            AP[h, k] = p
            WP[h, k] = p * k.astype(f32)
            KT[h, k] = jnp.sum(r * p, axis=0)

        loop(B + 1, powers)
        KT[h, 0] = KT[h, 0] + skipv[pl.ds(h * 8, 8), :]

    def to_tm(slot, dst, off):
        def step(i):
            v = nat[slot, pl.ds(pl.multiple_of(i * 16, 16), 16), :].astype(f32)
            dst[pl.ds(off + i * 16, 16)] = v.reshape(16, H, 8, 128)

        loop(rows // 16, step)

    in_copies[0].wait()
    to_tm(2, KX, 8)
    in_copies[1].wait()
    to_tm(3, VX, 8)
    in_copies[2].wait()
    to_tm(1, QX, 8)

    @pl.when(me > 0)
    def _():
        for copy in halo_copies:
            copy.wait_recv()

    @pl.when(me == 0)
    def _():
        halo[...] = jnp.zeros(halo.shape, bf16)

    for i, dst in enumerate((QX, KX, VX)):
        dst[pl.ds(0, 8)] = halo[i].astype(f32)[8:16].reshape(8, H, 8, 128)

    def window(src, b, h):
        return src[pl.ds(b * 8 + 2, 14), h]

    def fir(win, i, h):
        return total(SW[i, h, j][None] * win[HALO - j : HALO - j + 8] for j in range(KS))

    def feature(h):
        def step(b):
            at = pl.ds(b * 8, 8)
            f1 = fir(window(KX, b, h), 1, h)
            F1[at, h] = f1
            f2 = fir(window(VX, b, h), 2, h)
            F2[at, h] = f2
            U[at, h] = f1 * f2

        loop(rows // 8, step)

    loop(H, feature)

    def summary(h):
        a = AP[h, 1]

        def step(b, run):
            u = U[pl.ds(b * B, B), h]
            x = a * u[0][None] + u[1][None]
            for s in range(2, B):
                x = a * x + u[s][None]
            XB[h, b] = x
            return AP[h, B] * run + x

        S1[pl.ds(h * M, M)] = lax.fori_loop(0, nb, step, jnp.zeros((M, 8, 128), f32))

    loop(H, summary)

    def scatter(src, dst, size, at):
        def step(i):
            p = lax.rem(me + i, n)
            pltpu.make_async_remote_copy(
                src_ref=src.at[pl.ds(p * size, size)], dst_ref=dst.at[pl.ds(me * size, size)],
                send_sem=ssem.at[at], recv_sem=rsem.at[at],
                device_id=peer(p), device_id_type=MESH,
            ).start()

        loop(n, step, 1)
        mine = pl.ds(me * size, size)
        pltpu.make_async_copy(src.at[mine], dst.at[mine], rsem.at[at]).start()

    def spread(src, dst, size, at):
        mine = pl.ds(me * size, size)

        def step(i):
            p = lax.rem(me + i, n)
            pltpu.make_async_remote_copy(
                src_ref=src, dst_ref=dst.at[mine],
                send_sem=ssem.at[at], recv_sem=rsem.at[at],
                device_id=peer(p), device_id_type=MESH,
            ).start()

        loop(n, step, 1)
        pltpu.make_async_copy(src, dst.at[mine], rsem.at[at]).start()

    def arrived(dst, at):
        pltpu.make_async_copy(dst, dst, rsem.at[at]).wait()

    def sent(dst, size, at):
        part = dst.at[pl.ds(0, (n - 1) * size)]
        pltpu.make_async_copy(part, part, ssem.at[at]).wait()

    def scan(src, dst, backward):
        a = AT[pl.ds(me * k1, k1)]
        run = jnp.zeros((k1, 8, 128), f32)
        for i in range(n):
            d = n - 1 - i if backward else i
            at = pl.ds(d * k1, k1)
            dst[at] = run
            run = a * run + src[at]

    scatter(S1, R1, k1, 0)

    def feature_q(h):
        def step(b):
            F0[pl.ds(b * 8, 8), h] = fir(window(QX, b, h), 0, h)

        loop(rows // 8, step)

    loop(H, feature_q)

    def inside(h):
        def step(b):
            u = [U[b * B + t, h] for t in range(B)]
            kt = [KT[h, k] for k in range(B)]
            for t in range(B):
                Y[b * B + t, h] = total(kt[k] * u[t - k] for k in range(t + 1))

        loop(nb, step)

    loop(H, inside)
    arrived(R1, 0)
    scan(R1, E1, False)
    scatter(E1, X0, k1, 1)

    def weighted(h):
        def step(b):
            u = U[pl.ds(b * B, B), h]
            PB[h, b] = total_in_order([WP[h, B - s] * u[s][None] for s in range(B)])

        loop(nb, step)

    def total_in_order(terms):
        out = terms[0]
        for term in terms[1:]:
            out = out + term
        return out

    loop(H, weighted)
    in_copies[3].wait()
    to_tm(0, RS, 0)
    in_copies[4].wait()
    to_tm(4, CT, 0)
    arrived(X0, 1)

    def entry(h):
        def step(b, x):
            later = AP[h, B] * x + XB[h, b]
            XB[h, b] = x
            return later

        lax.fori_loop(0, nb, step, X0[pl.ds(h * M, M)])

    loop(H, entry)

    lane = lax.broadcasted_iota(jnp.int32, (B, 128), 1)
    sums[...] = jnp.zeros((B, 128), f32)

    def forward(b):
        squares = [None] * B
        inner = [None] * B
        for h in range(H):
            a = AP[h, 1]
            z = RT[h] * a * XB[h, b]
            gain = gainv[pl.ds(h * 8, 8), :]
            for i in range(B):
                t = b * B + i
                y = Y[t, h] + jnp.sum(z, axis=0)
                if i + 1 < B:
                    z = a * z
                Y[t, h] = y
                s = RS[t, h] + F0[t, h] * y
                RS[t, h] = s
                sq = s * s
                ip = CT[t, h] * gain * s
                squares[i] = sq if h == 0 else squares[i] + sq
                inner[i] = ip if h == 0 else inner[i] + ip

        def column(parts):
            return jnp.sum(jnp.stack(parts).reshape(B, 1024), axis=1, keepdims=True)

        now = jnp.where(lane == b, column(squares), sums[...])
        sums[...] = jnp.where(lane == nb + b, column(inner), now)

    loop(nb, forward)
    for i in range(1, ntp):
        p = lax.rem(mt + i, ntp)
        pltpu.make_async_remote_copy(
            src_ref=sums, dst_ref=tpr.at[mt], send_sem=ssem.at[8], recv_sem=rsem.at[8],
            device_id=(me, p), device_id_type=MESH,
        ).start()
    pltpu.make_async_copy(sums, tpr.at[mt], rsem.at[8]).start()
    pltpu.make_async_copy(tpr, tpr, rsem.at[8]).wait()
    tot = total(tpr[i] for i in range(ntp))
    inner_sum = pltpu.roll(tot, 128 - nb, 1)
    valid = lane < nb
    inv_all = lax.rsqrt(jnp.where(valid, tot, 1.0) / D + 1e-5)
    coef_all = inv_all * inv_all * inv_all * jnp.where(valid, inner_sum, 0.0) / D

    def spread_rows(b):
        at = pl.ds(b * B, B)
        for src, dst in ((inv_all, INVT), (coef_all, CFT)):
            col = jnp.sum(jnp.where(lane == b, src, 0.0), axis=1, keepdims=True)
            full = jnp.broadcast_to(col, (B, 128))
            dst[at] = jnp.broadcast_to(full[:, None, :], (B, 8, 128))

    loop(nb, spread_rows)

    def backward(h):
        a = AP[h, 1]

        def step(i, run):
            b = nb - 1 - i
            at = pl.ds(b * B, B)
            gain = gainv[pl.ds(h * 8, 8), :][None]
            gs = INVT[at] * (CT[at, h] * gain) - RS[at, h] * CFT[at]
            GS[at, h] = gs
            dz = gs * F0[at, h]
            DZ[at, h] = dz
            v = a * dz[B - 1][None] + dz[B - 2][None]
            for s in range(B - 3, -1, -1):
                v = a * v + dz[s][None]
            AB[h, b] = v
            return AP[h, B] * run + v

        S2[pl.ds(h * M, M)] = lax.fori_loop(0, nb, step, jnp.zeros((M, 8, 128), f32))

    def fix(h):
        backward(h)

    for h in range(H):
        fix(h)
    scatter(S2, R2, k1, 2)

    def store(slot, b, h, value):
        nat[slot, pl.ds(pl.multiple_of(b * 16, 16), 16), pl.ds(h * 1024, 1024)] = value.reshape(
            B, 1024
        ).astype(bf16)

    for h in range(H):

        def early(b, acc):
            at = pl.ds(b * B, B)
            gain = gainv[pl.ds(h * 8, 8), :][None]
            si = RS[at, h] * INVT[at]
            store(0, b, h, si * gain)
            gs = GS[at, h]
            store(4, b, h, gs)
            GF0[at, h] = gs * Y[at, h]
            return acc + jnp.sum(CT[at, h] * si, axis=0)

        T1[50 + h] = lax.fori_loop(0, nb, early, jnp.zeros((8, 128), f32))
    out_copies = [
        pltpu.make_async_copy(nat.at[slot], dst, outsem.at[i])
        for i, (slot, dst) in enumerate(
            ((0, normed_o), (4, gres_o), (1, gq_o), (2, gk_o), (3, gv_o))
        )
    ]
    out_copies[0].start()
    out_copies[1].start()

    def grad_halo(i, ref):
        return pltpu.make_async_remote_copy(
            src_ref=ref.at[pl.ds(0, HALO)], dst_ref=ref.at[pl.ds(rows, HALO)],
            send_sem=hssem.at[3 + i], recv_sem=hrsem.at[3 + i],
            device_id=peer(lax.rem(me + n - 1, n)), device_id_type=MESH,
        )

    grad_copies = [grad_halo(i, ref) for i, ref in enumerate((GF0, GF1, GF2))]

    @pl.when(me > 0)
    def _():
        grad_copies[0].start()

    def correlate(h):
        def step(b, acc):
            u = [U[b * B + t, h] for t in range(B)]
            dz = [DZ[b * B + t, h] for t in range(B)]
            return tuple(
                acc[k] + total(dz[t] * u[t - k] for t in range(k, B)) for k in range(B)
            )

        zero = jnp.zeros((8, 128), f32)
        out = lax.fori_loop(0, nb, step, (zero,) * B)
        for k in range(B):
            CK[h, k] = out[k]

    loop(H, correlate)
    arrived(R2, 2)
    scan(R2, E2, True)
    scatter(E2, A0, k1, 3)

    def inside_back(h):
        def step(b):
            dz = [DZ[b * B + t, h] for t in range(B)]
            kt = [KT[h, k] for k in range(B)]
            for s in range(B):
                G[b * B + s, h] = total(kt[k] * dz[s + k] for k in range(B - s))

        loop(nb, step)

    loop(H, inside_back)

    def mode_sums(h):
        def step(b):
            dz = DZ[pl.ds(b * B, B), h]
            x = XB[h, b]
            RA[h] = RA[h] + x * AB[h, b]
            q = total_in_order([WP[h, s] * dz[s][None] for s in range(1, B)])
            SA[h] = SA[h] + x * q

        RA[h] = jnp.zeros((M, 8, 128), f32)
        SA[h] = jnp.zeros((M, 8, 128), f32)
        loop(nb, step)
        a = AP[h, 1]
        gr = a * RA[h]
        gl = a * SA[h]
        for k in range(B):
            c = CK[h, k][None]
            gr = gr + AP[h, k] * c
            gl = gl + WP[h, k] * c
        T1[pl.ds(h * M, M)] = gr
        SA[h] = gl
        T1[48 + h] = CK[h, 0]

    loop(H, mode_sums)

    def filter_sums(src, gf, dst, base):
        def half(h):
            def step(b, acc):
                win = window(src, b, h)
                g = gf[pl.ds(b * 8, 8), h]
                return tuple(
                    acc[j] + jnp.sum(g * win[HALO - j : HALO - j + 8], axis=0) for j in range(KS)
                )

            zero = jnp.zeros((8, 128), f32)
            out = lax.fori_loop(0, rows // 8, step, (zero,) * KS)
            for j in range(KS):
                dst[base + h * 8 + j] = out[j]
            dst[base + h * 8 + KS] = zero

        loop(H, half)

    filter_sums(QX, GF0, T1, 32)
    T1[pl.ds(48 + 2 + H, 16 - 2 - H)] = jnp.zeros((16 - 2 - H, 8, 128), f32)
    scatter(T1, RR1, k2, 4)

    @pl.when(me == n - 1)
    def _():
        for ref in (GF0, GF1, GF2):
            ref[pl.ds(rows, 8)] = jnp.zeros((8, H, 8, 128), f32)

    @pl.when(me < n - 1)
    def _():
        grad_copies[0].wait_recv()

    def back_filter(gf, i, slot):
        for h in range(H):

            def step(b):
                win = gf[pl.ds(b * B, B + HALO), h]
                store(slot, b, h, total(SW[i, h, j][None] * win[j : j + B] for j in range(KS)))

            loop(nb, step)

    back_filter(GF0, 0, 1)
    out_copies[2].start()
    arrived(A0, 3)

    def exits(h):
        def step(i, x):
            b = nb - 1 - i
            earlier = AP[h, B] * x + AB[h, b]
            AB[h, b] = x
            return earlier

        lax.fori_loop(0, nb, step, A0[pl.ds(h * M, M)])

    loop(H, exits)

    def mixed(b):
        for h in range(H):
            a = AP[h, 1]
            out = AB[h, b]
            SA[h] = SA[h] + out * (PB[h, b] + (float(B) * a) * AP[h, B] * XB[h, b])
            z = RT[h] * a * out
            for i in range(B):
                t = b * B + (B - 1 - i)
                g = G[t, h] + jnp.sum(z, axis=0)
                if i + 1 < B:
                    z = a * z
                GF1[t, h] = g * F2[t, h]
                GF2[t, h] = g * F1[t, h]

    mixed(0)

    @pl.when(me > 0)
    def _():
        grad_copies[1].start()
        grad_copies[2].start()

    loop(nb, mixed, 1)
    arrived(RR1, 4)

    def reduce(src, dst):
        dst[...] = total(src[pl.ds(i * k2, k2)] for i in range(n))

    reduce(RR1, SUM1)
    spread(SUM1, AG1, k2, 5)
    for h in range(H):
        T2[pl.ds(h * M, M)] = -RT[h] * SA[h]
    filter_sums(KX, GF1, T2, 32)
    filter_sums(VX, GF2, T2, 48)
    scatter(T2, RR2, k2, 6)

    @pl.when(me < n - 1)
    def _():
        grad_copies[1].wait_recv()
        grad_copies[2].wait_recv()

    back_filter(GF1, 1, 2)
    out_copies[3].start()
    arrived(RR2, 6)
    reduce(RR2, SUM2)
    spread(SUM2, AG2, k2, 7)
    back_filter(GF2, 2, 3)
    out_copies[4].start()

    def natural(src, at, count):
        return src[pl.ds(at, count)].reshape(count, 1024)

    arrived(AG1, 5)
    for h in range(H):
        cols = pl.ds(h * 1024, 1024)
        grv[:, cols] = natural(AG1, h * M, M)
        shv[0, :, cols] = natural(AG1, 32 + h * 8, 8)[0:KS]
        skipv[pl.ds(h * 8, 8), :] = AG1[48 + h]
        gainv[pl.ds(h * 8, 8), :] = AG1[50 + h]
    arrived(AG2, 7)
    for h in range(H):
        cols = pl.ds(h * 1024, 1024)
        glv[:, cols] = natural(AG2, h * M, M)
        shv[1, :, cols] = natural(AG2, 32 + h * 8, 8)[0:KS]
        shv[2, :, cols] = natural(AG2, 48 + h * 8, 8)[0:KS]
    small = [
        pltpu.make_async_copy(s, d, outsem.at[5 + i])
        for i, (s, d) in enumerate(
            ((shv, short_o), (grv, gr_o), (glv, gl_o), (skipv, gskip_o), (gainv, ggain_o))
        )
    ]
    for copy in small:
        copy.start()

    for at, dst, size in (
        (0, R1, k1), (1, X0, k1), (2, R2, k1), (3, A0, k1),
        (4, RR1, k2), (5, AG1, k2), (6, RR2, k2), (7, AG2, k2),
    ):
        sent(dst, size, at)
    part = tpr.at[pl.ds(0, ntp - 1)]
    pltpu.make_async_copy(part, part, ssem.at[8]).wait()

    @pl.when(me < n - 1)
    def _():
        for copy in halo_copies:
            copy.wait_send()

    @pl.when(me > 0)
    def _():
        for copy in grad_copies:
            copy.wait_send()

    for copy in out_copies + small:
        copy.wait()


def shards(
    n, ntp, residual, query_in, key_in, value_in, short_filter, residues, decay_rate, skip_gain,
    norm_gain, cotangent,
):
    rows, width = residual.shape
    H = width // 1024
    nb = rows // B
    tiles = H * M

    def V(*shape, dtype=f32):
        return pltpu.VMEM(shape, dtype)

    def tm(extra=0):
        return V(rows + extra, H, 8, 128)

    def tile(count):
        return V(count, 8, 128)

    k1, k2 = tiles // n, 64 // n
    scratch = (
        [V(5, rows, width, dtype=bf16), V(3, 16, width, dtype=bf16)]
        + [V(3, KS, width), V(M, width), V(M, width), V(H * 8, 128), V(H * 8, 128)]
        + [tm(8)] * 3 + [tm()] * 10 + [tm(8)] * 3
        + [V(H, B + 1, M, 8, 128)] * 2
        + [V(H, B + 1, 8, 128), V(H, M, 8, 128), V(3, H, 8, 8, 128), tile(tiles)]
        + [V(H, nb, M, 8, 128)] * 3
        + [tile(tiles)] * 8
        + [V(B, 128), V(ntp, B, 128), tile(rows), tile(rows)]
        + [V(H, M, 8, 128), V(H, M, 8, 128), V(H, B, 8, 128), V(8, 1024)]
        + [tile(64), tile(64), tile(k2), tile(64)] * 2
        + [V(3, KS, width), V(M, width), V(M, width)]
        + [pltpu.SemaphoreType.DMA((c,)) for c in (10, 10, 9, 9, 6, 6)]
    )
    big = jax.ShapeDtypeStruct((rows, width), bf16)
    vec = jax.ShapeDtypeStruct((H * 8, 128), f32)
    out_shape = (
        [big] * 5
        + [jax.ShapeDtypeStruct((3, KS, width), f32)]
        + [jax.ShapeDtypeStruct((M, width), f32)] * 2
        + [vec, vec]
    )
    anywhere = pl.BlockSpec(memory_space=pl.ANY)
    outs = pl.pallas_call(
        functools.partial(kernel, n, ntp, rows, width),
        out_shape=out_shape,
        in_specs=[anywhere] * 10,
        out_specs=[anywhere] * 10,
        scratch_shapes=scratch,
        compiler_params=pltpu.CompilerParams(
            collective_id=0, has_side_effects=True, vmem_limit_bytes=60 << 20
        ),
    )(
        residual, query_in, key_in, value_in, short_filter, residues, decay_rate,
        skip_gain.reshape(H * 8, 128), norm_gain.reshape(H * 8, 128), cotangent,
    )
    return (*outs[:8], outs[8].reshape(width), outs[9].reshape(width))


def solution(mesh):
    act, par, vec = P("ctx", "tp"), P(None, "tp"), P("tp")
    short = P(None, None, "tp")
    return jax.shard_map(
        functools.partial(shards, mesh.shape["ctx"], mesh.shape["tp"]),
        mesh=mesh,
        in_specs=(act, act, act, act, short, par, par, vec, vec, act),
        out_specs=(act, act, act, act, act, short, par, par, vec, vec),
        check_vma=False,
    )
```

time: 969 us -> 91.4 us (0.09); the launches traced: 954 us -> 90.9 us
  other arithmetic: 409 us -> 0 us
  blocking collectives: 199 us -> 0 us
  waiting for transfers between devices: 107 us -> 0 us
  local copies, waits for them, and re-layouts: 112 us -> 12.2 us
  Pallas kernels: 0 us -> 78 us
  matrix products: 50.2 us -> 0 us
  loops' own time: 48.4 us -> 0 us
  between operations: 15.1 us -> 0.68 us
  starting transfers between devices: 12.7 us -> 0 us
    dot_general x81 -> x0, other arithmetic: 220 us -> none  [the longest x8 38.3 us: output_advance(): inside = jnp.einsum('tsc,sc->tc', toeplitz, u_block, precision=exact_mode)]
    psum x3 -> x0, blocking collectives: 137 us -> none  [the longest x1 122 us: shards(): lax.psum((local_short, sum_res, residues * sum_rate, local_skip, local_ga...]
    psum x1 -> x0, waiting for transfers between devices: 84.2 us -> none  [shards(): lax.psum((local_short, sum_res, residues * sum_rate, local_skip, local_ga...]
    pallas_call x0 -> x1, Pallas kernels: none -> 78 us  [shards(): pl.pallas_call(functools.partial(kernel, n, ntp, rows, width), out_shape=...]
    select_n x62 -> x0, other arithmetic: 62.8 us -> none  [lap(): jnp.where(position < mine, new, old)]
    unnamed x1 -> x0, blocking collectives: 62.2 us -> none
    dot_general x9 -> x0, matrix products: 50.2 us -> none  [the longest x8 44.6 us: gradient_advance(): lagged = jnp.einsum('tsk,tsc->kc', shifter, products, precision=exact_mode)]
    another operation x7 -> x0, loops' own time: 48.4 us -> none  [the longest x2 41.9 us: prefix(): return lax.fori_loop(0, count - 1, lap, so_far)]
  transfers between devices with their start and end apart: 6 -> 0, of which waited for: 2 -> 0; matrix products, arithmetic and copies ran while one was open for 15% -> 0% of each run, Pallas kernels for 0% -> 0%
where the time goes in v1:
time: 91.4 us; the launch traced here: 90.9 us
  Pallas kernels  78 us (85%)
  local copies, waits for them, and re-layouts  12.2 us (13%)
    pallas_call x1, Pallas kernels, shards(): pl.pallas_call(functools.partial(kernel, n, ntp, rows, width), out_shape=...  78 us
    unnamed x28, local copies, waits for them, and re-layouts  12.2 us

profile of v1, /device:TPU:1, one launch (start us, length us, event | category | flops | bytes accessed | tf_op | source)
XLA Modules:
  0.0 90.9 jit_solution(1367136024601189714)
XLA Ops:
  0.6 78.0 %shard_map.177 = (bf16[256,2048]{1,0:T(8,128)(2,1)}, bf16[256,2048]{1,0:T(8,128)(2,1)}, bf16[256,2048]{1,0:T(8,128)(2,1)}, bf16[256,2048]{1,0:T(8,128)(2,1)}, bf...) custom-call(bf16[256,2048]{1,0:T(8,128)(2,1)} %res_h.1, ...), custom_call_target="tpu_custom_call" | custom-call | tf_op jit(solution)/shard_map/pallas_call | solution.py:640
  78.7 0.0 copy-start.3
  78.7 2.4 %copy.30 = bf16[256,2048]{1,0:T(8,128)(2,1)} copy(bf16[256,2048]{1,0:T(8,128)(2,1)} %get-tuple-element.40) | data formatting | bytes 2097152
  81.1 0.0 copy-done.3
  81.1 0.0 copy-start.2
  81.1 1.0 %copy.31 = bf16[256,2048]{1,0:T(8,128)(2,1)} copy(bf16[256,2048]{1,0:T(8,128)(2,1)S(1)} %copy-done.3) | data formatting | bytes 2097152
  82.0 0.6 copy-done.2
  82.7 0.0 copy-start.1
  82.7 1.0 %copy.32 = bf16[256,2048]{1,0:T(8,128)(2,1)} copy(bf16[256,2048]{1,0:T(8,128)(2,1)S(1)} %copy-done.2) | data formatting | bytes 2097152
  83.6 0.6 copy-done.1
  84.3 0.0 copy-start
  84.3 1.0 %copy.33 = bf16[256,2048]{1,0:T(8,128)(2,1)} copy(bf16[256,2048]{1,0:T(8,128)(2,1)S(1)} %copy-done.1) | data formatting | bytes 2097152
  85.2 0.6 copy-done
  85.9 0.0 copy-start.4
  85.9 1.0 %copy.34 = bf16[256,2048]{1,0:T(8,128)(2,1)} copy(bf16[256,2048]{1,0:T(8,128)(2,1)S(1)} %copy-done) | data formatting | bytes 2097152
  86.8 0.1 copy-done.4
  87.0 0.0 copy-start.6
  87.0 0.7 copy.35
  87.7 0.3 copy-done.6
  88.0 0.0 copy-start.5
  88.0 0.7 copy.36
  88.6 0.3 copy-done.5
  88.9 0.0 copy-start.8
  88.9 0.7 copy.37
  89.6 0.0 copy-done.8
  89.6 0.0 copy-start.7
  89.6 0.6 copy.38
  90.2 0.1 copy-done.7
  90.3 0.6 copy.39
Async XLA Ops:
  78.7 2.4 %copy-start.3 = (bf16[256,2048]{1,0:T(8,128)(2,1)S(1)}, bf16[256,2048]{1,0:T(8,128)(2,1)}, u32[]{:S(2)}) copy-start(bf16[256,2048]{1,0:T(8,128)(2,1)} %get-tuple-element.41) | copy-start | bytes 3145732
  81.1 1.6 %copy-start.2 = (bf16[256,2048]{1,0:T(8,128)(2,1)S(1)}, bf16[256,2048]{1,0:T(8,128)(2,1)}, u32[]{:S(2)}) copy-start(bf16[256,2048]{1,0:T(8,128)(2,1)} %get-tuple-element.42) | copy-start | bytes 3145732
  82.7 1.6 %copy-start.1 = (bf16[256,2048]{1,0:T(8,128)(2,1)S(1)}, bf16[256,2048]{1,0:T(8,128)(2,1)}, u32[]{:S(2)}) copy-start(bf16[256,2048]{1,0:T(8,128)(2,1)} %get-tuple-element.43) | copy-start | bytes 3145732
  84.3 1.6 %copy-start = (bf16[256,2048]{1,0:T(8,128)(2,1)S(1)}, bf16[256,2048]{1,0:T(8,128)(2,1)}, u32[]{:S(2)}) copy-start(bf16[256,2048]{1,0:T(8,128)(2,1)} %get-tuple-element.44) | copy-start | bytes 3145732
  85.9 1.1 %copy-start.4 = (f32[3,7,2048]{2,1,0:T(8,128)S(1)}, f32[3,7,2048]{2,1,0:T(8,128)}, u32[]{:S(2)}) copy-start(f32[3,7,2048]{2,1,0:T(8,128)} %get-tuple-element.45) | copy-start | bytes 516100
  87.0 1.0 %copy-start.6 = (f32[16,2048]{1,0:T(8,128)S(1)}, f32[16,2048]{1,0:T(8,128)}, u32[]{:S(2)}) copy-start(f32[16,2048]{1,0:T(8,128)} %get-tuple-element.46) | copy-start | bytes 393220
  88.0 1.0 %copy-start.5 = (f32[16,2048]{1,0:T(8,128)S(1)}, f32[16,2048]{1,0:T(8,128)}, u32[]{:S(2)}) copy-start(f32[16,2048]{1,0:T(8,128)} %get-tuple-element.47) | copy-start | bytes 393220
  88.9 0.7 copy-start.8
  89.6 0.7 copy-start.7

commit v2 on v1

--- a/solution.py
+++ b/solution.py
@@ -38,14 +38,13 @@
     n, ntp, rows, width,
     res_h, q_h, k_h, v_h, sf_h, r_h, lam_h, skip_h, gain_h, cot_h,
     normed_o, gres_o, gq_o, gk_o, gv_o, short_o, gr_o, gl_o, gskip_o, ggain_o,
-    nat, halo, sfv, rv, lv, skipv, gainv,
+    halo, sfv, rv, lv, skipv, gainv,
     QX, KX, VX, RS, CT, F0, F1, F2, U, Y, DZ, GS, G, GF0, GF1, GF2,
     AP, WP, KT, RT, SW, AT, XB, PB, AB,
     S1, R1, E1, X0, S2, R2, E2, A0,
     sums, tpr, INVT, CFT, RA, SA, CK, SG,
     T1, RR1, SUM1, AG1, T2, RR2, SUM2, AG2,
-    shv, grv, glv,
-    insem, outsem, ssem, rsem, hssem, hrsem,
+    insem, ssem, rsem, hssem, hrsem,
 ):
     H = width // 1024
     nb = rows // B
@@ -59,8 +58,10 @@
     def peer(p):
         return (p, mt)
 
+    nat = (normed_o, gq_o, gk_o, gv_o, gres_o)
+
     ins = [
-        (k_h, nat.at[2]), (v_h, nat.at[3]), (q_h, nat.at[1]), (res_h, nat.at[0]), (cot_h, nat.at[4]),
+        (k_h, nat[2]), (v_h, nat[3]), (q_h, nat[1]), (res_h, nat[0]), (cot_h, nat[4]),
         (sf_h, sfv), (r_h, rv), (lam_h, lv), (skip_h, skipv), (gain_h, gainv),
     ]
     in_copies = [pltpu.make_async_copy(s, d, insem.at[i]) for i, (s, d) in enumerate(ins)]
@@ -119,7 +120,7 @@
 
     def to_tm(slot, dst, off):
         def step(i):
-            v = nat[slot, pl.ds(pl.multiple_of(i * 16, 16), 16), :].astype(f32)
+            v = nat[slot][pl.ds(pl.multiple_of(i * 16, 16), 16), :].astype(f32)
             dst[pl.ds(off + i * 16, 16)] = v.reshape(16, H, 8, 128)
 
         loop(rows // 16, step)
@@ -354,7 +355,7 @@
     scatter(S2, R2, k1, 2)
 
     def store(slot, b, h, value):
-        nat[slot, pl.ds(pl.multiple_of(b * 16, 16), 16), pl.ds(h * 1024, 1024)] = value.reshape(
+        nat[slot][pl.ds(pl.multiple_of(b * 16, 16), 16), pl.ds(h * 1024, 1024)] = value.reshape(
             B, 1024
         ).astype(bf16)
 
@@ -371,15 +372,6 @@
             return acc + jnp.sum(CT[at, h] * si, axis=0)
 
         T1[50 + h] = lax.fori_loop(0, nb, early, jnp.zeros((8, 128), f32))
-    out_copies = [
-        pltpu.make_async_copy(nat.at[slot], dst, outsem.at[i])
-        for i, (slot, dst) in enumerate(
-            ((0, normed_o), (4, gres_o), (1, gq_o), (2, gk_o), (3, gv_o))
-        )
-    ]
-    out_copies[0].start()
-    out_copies[1].start()
-
     def grad_halo(i, ref):
         return pltpu.make_async_remote_copy(
             src_ref=ref.at[pl.ds(0, HALO)], dst_ref=ref.at[pl.ds(rows, HALO)],
@@ -486,7 +478,6 @@
             loop(nb, step)
 
     back_filter(GF0, 0, 1)
-    out_copies[2].start()
     arrived(A0, 3)
 
     def exits(h):
@@ -541,12 +532,10 @@
         grad_copies[2].wait_recv()
 
     back_filter(GF1, 1, 2)
-    out_copies[3].start()
     arrived(RR2, 6)
     reduce(RR2, SUM2)
     spread(SUM2, AG2, k2, 7)
     back_filter(GF2, 2, 3)
-    out_copies[4].start()
 
     def natural(src, at, count):
         return src[pl.ds(at, count)].reshape(count, 1024)
@@ -554,24 +543,16 @@
     arrived(AG1, 5)
     for h in range(H):
         cols = pl.ds(h * 1024, 1024)
-        grv[:, cols] = natural(AG1, h * M, M)
-        shv[0, :, cols] = natural(AG1, 32 + h * 8, 8)[0:KS]
-        skipv[pl.ds(h * 8, 8), :] = AG1[48 + h]
-        gainv[pl.ds(h * 8, 8), :] = AG1[50 + h]
+        gr_o[:, cols] = natural(AG1, h * M, M)
+        short_o[0, :, cols] = natural(AG1, 32 + h * 8, 8)[0:KS]
+        gskip_o[pl.ds(h * 8, 8), :] = AG1[48 + h]
+        ggain_o[pl.ds(h * 8, 8), :] = AG1[50 + h]
     arrived(AG2, 7)
     for h in range(H):
         cols = pl.ds(h * 1024, 1024)
-        glv[:, cols] = natural(AG2, h * M, M)
-        shv[1, :, cols] = natural(AG2, 32 + h * 8, 8)[0:KS]
-        shv[2, :, cols] = natural(AG2, 48 + h * 8, 8)[0:KS]
-    small = [
-        pltpu.make_async_copy(s, d, outsem.at[5 + i])
-        for i, (s, d) in enumerate(
-            ((shv, short_o), (grv, gr_o), (glv, gl_o), (skipv, gskip_o), (gainv, ggain_o))
-        )
-    ]
-    for copy in small:
-        copy.start()
+        gl_o[:, cols] = natural(AG2, h * M, M)
+        short_o[1, :, cols] = natural(AG2, 32 + h * 8, 8)[0:KS]
+        short_o[2, :, cols] = natural(AG2, 48 + h * 8, 8)[0:KS]
 
     for at, dst, size in (
         (0, R1, k1), (1, X0, k1), (2, R2, k1), (3, A0, k1),
@@ -591,7 +572,13 @@
         for copy in grad_copies:
             copy.wait_send()
 
-    for copy in out_copies + small:
+
+def deliver(*refs):
+    ins, outs, sem = refs[:10], refs[10:20], refs[20]
+    copies = [pltpu.make_async_copy(s, d, sem.at[i]) for i, (s, d) in enumerate(zip(ins, outs))]
+    for copy in copies:
+        copy.start()
+    for copy in copies:
         copy.wait()
 
 
@@ -615,7 +602,7 @@
 
     k1, k2 = tiles // n, 64 // n
     scratch = (
-        [V(5, rows, width, dtype=bf16), V(3, 16, width, dtype=bf16)]
+        [V(3, 16, width, dtype=bf16)]
         + [V(3, KS, width), V(M, width), V(M, width), V(H * 8, 128), V(H * 8, 128)]
         + [tm(8)] * 3 + [tm()] * 10 + [tm(8)] * 3
         + [V(H, B + 1, M, 8, 128)] * 2
@@ -625,8 +612,7 @@
         + [V(B, 128), V(ntp, B, 128), tile(rows), tile(rows)]
         + [V(H, M, 8, 128), V(H, M, 8, 128), V(H, B, 8, 128), V(8, 1024)]
         + [tile(64), tile(64), tile(k2), tile(64)] * 2
-        + [V(3, KS, width), V(M, width), V(M, width)]
-        + [pltpu.SemaphoreType.DMA((c,)) for c in (10, 10, 9, 9, 6, 6)]
+        + [pltpu.SemaphoreType.DMA((c,)) for c in (10, 9, 9, 6, 6)]
     )
     big = jax.ShapeDtypeStruct((rows, width), bf16)
     vec = jax.ShapeDtypeStruct((H * 8, 128), f32)
@@ -639,17 +625,25 @@
     anywhere = pl.BlockSpec(memory_space=pl.ANY)
     outs = pl.pallas_call(
         functools.partial(kernel, n, ntp, rows, width),
-        out_shape=out_shape,
+        out_shape=[V(*o.shape, dtype=o.dtype) for o in out_shape],
         in_specs=[anywhere] * 10,
-        out_specs=[anywhere] * 10,
+        out_specs=[pl.BlockSpec(memory_space=pltpu.VMEM)] * 10,
         scratch_shapes=scratch,
         compiler_params=pltpu.CompilerParams(
-            collective_id=0, has_side_effects=True, vmem_limit_bytes=60 << 20
+            collective_id=0, has_side_effects=True, vmem_limit_bytes=52 << 20
         ),
     )(
         residual, query_in, key_in, value_in, short_filter, residues, decay_rate,
         skip_gain.reshape(H * 8, 128), norm_gain.reshape(H * 8, 128), cotangent,
     )
+    outs = pl.pallas_call(
+        deliver,
+        out_shape=out_shape,
+        in_specs=[anywhere] * 10,
+        out_specs=[anywhere] * 10,
+        scratch_shapes=[pltpu.SemaphoreType.DMA((10,))],
+        compiler_params=pltpu.CompilerParams(vmem_limit_bytes=1 << 20),
+    )(*outs)
     return (*outs[:8], outs[8].reshape(width), outs[9].reshape(width))
 
 

time: 91.4 us -> 80.5 us (0.88)
  local copies, waits for them, and re-layouts: 12.2 us -> 0 us
  Pallas kernels: 78 us -> 79.7 us
    unnamed x28 -> x0, local copies, waits for them, and re-layouts: 12.2 us -> none
    pallas_call x0 -> x1, Pallas kernels: none -> 2.55 us  [shards(): pl.pallas_call(deliver, out_shape=out_shape, in_specs=[anywhere] * 10, ou...]
where the time goes in v2:
time: 80.5 us; the launch traced here: 80.4 us
  Pallas kernels  79.7 us (99%)
    pallas_call x1, Pallas kernels, shards(): pl.pallas_call(functools.partial(kernel, n, ntp, rows, width), out_shape=...  77.2 us
    pallas_call x1, Pallas kernels, shards(): pl.pallas_call(deliver, out_shape=out_shape, in_specs=[anywhere] * 10, ou...  2.55 us

profile of v2, /device:TPU:1, one launch (start us, length us, event | category | flops | bytes accessed | tf_op | source)
XLA Modules:
  0.0 80.4 jit_solution(10747833506366775306)
XLA Ops:
  0.6 77.2 %shard_map.177 = (bf16[256,2048]{1,0:T(8,128)(2,1)S(1)}, bf16[256,2048]{1,0:T(8,128)(2,1)S(1)}, bf16[256,2048]{1,0:T(8,128)(2,1)S(1)}, bf16[256,2048]{1,0:T(8,12...) custom-call(bf16[256,2048]{1,0:T(8,128)(2,1)} %res_h.1, ...), custom_call_target="tpu_custom_call" | custom-call | tf_op jit(solution)/shard_map/pallas_call | solution.py:626
  77.8 2.5 %shard_map.178 = (bf16[256,2048]{1,0:T(8,128)(2,1)}, bf16[256,2048]{1,0:T(8,128)(2,1)}, bf16[256,2048]{1,0:T(8,128)(2,1)}, bf16[256,2048]{1,0:T(8,128)(2,1)}, bf...) custom-call(bf16[256,2048]{1,0:T(8,128)(2,1)S(1)} %get-tuple-element, ...), custom_call_target="tpu_custom_call" | custom-call | tf_op jit(solution)/shard_map/pallas_call | solution.py:639

commit v3 on v2

v3 whole, which is shorter than its diff:
```python
import functools

import jax
import jax.numpy as jnp
from jax import lax
from jax.experimental import pallas as pl
from jax.experimental.pallas import tpu as pltpu
from jax.sharding import PartitionSpec as P

f32 = jnp.float32
bf16 = jnp.bfloat16
MESH = pl.DeviceIdType.MESH
B = 16
M = 16
KS = 7
HALO = KS - 1


def loop(count, step, start=0):
    def lap(i, carry):
        step(i)
        return carry

    lax.fori_loop(start, count, lap, 0)


def total(terms):
    terms = list(terms)
    while len(terms) > 1:
        terms = [
            terms[i] + terms[i + 1] if i + 1 < len(terms) else terms[i]
            for i in range(0, len(terms), 2)
        ]
    return terms[0]


def kernel(
    n, ntp, rows, width,
    res_h, q_h, k_h, v_h, sf_h, r_h, lam_h, skip_h, gain_h, cot_h,
    normed_o, gres_o, gq_o, gk_o, gv_o, short_o, gr_o, gl_o, gskip_o, ggain_o,
    halo, sfv, rv, lv, skipv, gainv,
    QX, KX, VX, RS, CT, F0, F1, F2, U, Y, DZ, GS, G, GF0, GF1, GF2,
    AP, WP, KT, RT, LM, SW, AT, XB, PB, AB,
    S1, R1, E1, X0, S2, R2, E2, A0,
    sums, tpr, INVT, CFT, RA, SA, QA, CK, SG,
    T1, RR1, SUM1, AG1, T2, RR2, SUM2, AG2,
    insem, ssem, rsem, hssem, hrsem,
):
    H = width // 1024
    nb = rows // B
    D = width * ntp
    me = lax.axis_index("ctx")
    mt = lax.axis_index("tp")
    tiles = H * M
    k1 = tiles // n
    k2 = 64 // n
    k3 = 32 // n

    def peer(p):
        return (p, mt)

    nat = (normed_o, gq_o, gk_o, gv_o, gres_o)

    ins = [
        (lam_h, lv), (sf_h, sfv), (k_h, nat[2]), (v_h, nat[3]), (r_h, rv), (skip_h, skipv),
        (gain_h, gainv), (q_h, nat[1]), (res_h, nat[0]), (cot_h, nat[4]),
    ]
    in_copies = [pltpu.make_async_copy(s, d, insem.at[i]) for i, (s, d) in enumerate(ins)]
    for copy in in_copies:
        copy.start()

    barrier = pltpu.get_barrier_semaphore()

    for i in range(1, n):
        pl.semaphore_signal(
            barrier, inc=1, device_id=peer(lax.rem(me + i, n)), device_id_type=MESH
        )
    for i in range(1, ntp):
        pl.semaphore_signal(
            barrier, inc=1, device_id=(me, lax.rem(mt + i, ntp)), device_id_type=MESH
        )

    in_copies[0].wait()
    in_copies[1].wait()
    for h in range(H):
        cols = pl.ds(h * 1024, 1024)
        lam = lv[:, cols].reshape(M, 8, 128)
        AP[h, 1] = jnp.exp(-lam)
        AP[h, B] = jnp.exp(lam * (-float(B)))
        LM[h] = lam
        AT[pl.ds(h * M, M)] = jnp.exp(lam * (-float(rows)))
        for i in range(3):
            SG[0:8, :] = jnp.zeros((8, 1024), f32)
            SG[0:KS, :] = sfv[i, :, cols]
            SW[i, h] = SG[0:8, :].reshape(8, 8, 128)

    def to_tm(slot, dst, off):
        def step(i):
            v = nat[slot][pl.ds(pl.multiple_of(i * 16, 16), 16), :].astype(f32)
            dst[pl.ds(off + i * 16, 16)] = v.reshape(16, H, 8, 128)

        loop(rows // 16, step)

    in_copies[2].wait()
    to_tm(2, KX, 8)
    in_copies[3].wait()
    to_tm(3, VX, 8)

    pl.semaphore_wait(barrier, n - 1 + ntp - 1)

    def in_halo(i, src):
        return pltpu.make_async_remote_copy(
            src_ref=src.at[pl.ds(rows - 16, 16)], dst_ref=halo.at[i],
            send_sem=hssem.at[i], recv_sem=hrsem.at[i],
            device_id=peer(lax.rem(me + 1, n)), device_id_type=MESH,
        )

    halo_copies = [in_halo(0, q_h), in_halo(1, k_h), in_halo(2, v_h)]

    @pl.when(me < n - 1)
    def _():
        for i in (1, 2, 0):
            halo_copies[i].start()

    def window(src, b, h):
        return src[pl.ds(b * 8 + 2, 14), h]

    def fir(win, i, h):
        return total(SW[i, h, j][None] * win[HALO - j : HALO - j + 8] for j in range(KS))

    def feature(h, b):
        at = pl.ds(b * 8, 8)
        f1 = fir(window(KX, b, h), 1, h)
        F1[at, h] = f1
        f2 = fir(window(VX, b, h), 2, h)
        F2[at, h] = f2
        U[at, h] = f1 * f2

    def gather(h, b):
        a = AP[h, 1]
        u = U[pl.ds(b * B, B), h]
        x = a * u[0][None] + u[1][None]
        for s in range(2, B):
            x = a * x + u[s][None]
        XB[h, b] = x
        return x

    def summary(h):
        def step(b, run):
            return AP[h, B] * run + gather(h, b)

        S1[pl.ds(h * M, M)] = lax.fori_loop(1, nb, step, jnp.zeros((M, 8, 128), f32))

    for h in range(H):
        loop(rows // 8, functools.partial(feature, h), 1)
    loop(H, summary)

    @pl.when(me > 0)
    def _():
        for i in (1, 2, 0):
            halo_copies[i].wait_recv()

    @pl.when(me == 0)
    def _():
        halo[...] = jnp.zeros(halo.shape, bf16)

    for i, dst in enumerate((QX, KX, VX)):
        dst[pl.ds(0, 8)] = halo[i].astype(f32)[8:16].reshape(8, H, 8, 128)

    half = n // H

    def remote(src, dst, p, at):
        pltpu.make_async_remote_copy(
            src_ref=src, dst_ref=dst, send_sem=ssem.at[at[0]], recv_sem=rsem.at[at[1]],
            device_id=peer(p), device_id_type=MESH,
        ).start()

    def part(ref, p, size):
        return ref.at[pl.ds(p * size, size)]

    def scatter(src, dst, size, at):
        mine = part(dst, me, size)
        for i in range(1, n):
            p = lax.rem(me + i, n)
            remote(part(src, p, size), mine, p, at)
        pltpu.make_async_copy(part(src, me, size), mine, rsem.at[at[1]]).start()

    def scatter_half(src, dst, size, at, h):
        mine = part(dst, me, size)
        for i in range(1, half):
            p = h * half + lax.rem(me + i, half)
            remote(part(src, p, size), mine, p, at)
        first = me < half if h == 0 else me >= half
        other = me >= half if h == 0 else me < half

        @pl.when(first)
        def _():
            pltpu.make_async_copy(part(src, me, size), mine, rsem.at[at[1]]).start()

        @pl.when(other)
        def _():
            p = h * half + lax.rem(me, half)
            remote(part(src, p, size), mine, p, at)

    def spread(src, dst, size, at):
        mine = part(dst, me, size)
        for i in range(1, n):
            remote(src, mine, lax.rem(me + i, n), at)
        pltpu.make_async_copy(src, mine, rsem.at[at[1]]).start()

    def arrived(dst, at):
        pltpu.make_async_copy(dst, dst, rsem.at[at]).wait()

    def sent(dst, size, at):
        all_but_one = dst.at[pl.ds(0, (n - 1) * size)]
        pltpu.make_async_copy(all_but_one, all_but_one, ssem.at[at]).wait()

    def scan(src, dst, backward):
        a = AT[pl.ds(me * k1, k1)]
        run = jnp.zeros((k1, 8, 128), f32)
        for i in range(n):
            d = n - 1 - i if backward else i
            at = pl.ds(d * k1, k1)
            dst[at] = run
            run = a * run + src[at]

    def relay(src, mid, dst, at, backward, h):
        @pl.when(me < half if h == 0 else me >= half)
        def _():
            arrived(src, at[1])
            scan(src, mid, backward)
            scatter(mid, dst, k1, (at[0] + 1, at[1] + 1 + h))

    for h in range(H):
        feature(h, 0)
        S1[pl.ds(h * M, M)] = S1[pl.ds(h * M, M)] + gather(h, 0) * jnp.exp(
            LM[h] * (-float(rows - B))
        )
        scatter_half(S1, R1, k1, (0, 0), h)

    for i in (4, 5, 6):
        in_copies[i].wait()
    for h in range(H):
        r = rv[:, pl.ds(h * 1024, 1024)].reshape(M, 8, 128)
        RT[h] = r

        def powers(k):
            p = jnp.exp(LM[h] * (-k.astype(f32)))
            AP[h, k] = p
            WP[h, k] = p * k.astype(f32)
            KT[h, k] = jnp.sum(r * p, axis=0)

        loop(B + 1, powers)
        KT[h, 0] = KT[h, 0] + skipv[pl.ds(h * 8, 8), :]
        RA[h] = r * AP[h, 1]

    def inside(h):
        def step(b):
            u = [U[b * B + t, h] for t in range(B)]
            kt = [KT[h, k] for k in range(B)]
            for t in range(B):
                Y[b * B + t, h] = total(kt[k] * u[t - k] for k in range(t + 1))

        loop(nb, step)

    loop(H, inside)
    in_copies[7].wait()
    to_tm(1, QX, 8)
    relay(R1, E1, X0, (0, 0), False, 0)
    relay(R1, E1, X0, (0, 0), False, 1)

    def feature_q(h):
        def step(b):
            F0[pl.ds(b * 8, 8), h] = fir(window(QX, b, h), 0, h)

        loop(rows // 8, step)

    loop(H, feature_q)
    in_copies[8].wait()
    to_tm(0, RS, 0)
    in_copies[9].wait()
    to_tm(4, CT, 0)

    def total_in_order(terms):
        out = terms[0]
        for term in terms[1:]:
            out = out + term
        return out

    def weighted(h):
        edge = (float(B) * AP[h, 1]) * AP[h, B]

        def step(b):
            u = U[pl.ds(b * B, B), h]
            PB[h, b] = total_in_order(
                [edge * XB[h, b]] + [WP[h, B - s] * u[s][None] for s in range(B)]
            )

        loop(nb, step)

    lane = lax.broadcasted_iota(jnp.int32, (B, 128), 1)
    sums[...] = jnp.zeros((B, 128), f32)

    def column(parts):
        return jnp.sum(jnp.stack(parts).reshape(B, 1024), axis=1, keepdims=True)

    def forward(h, b, x):
        a = AP[h, 1]
        z = RA[h] * x
        later = AP[h, B] * x + XB[h, b]
        XB[h, b] = x
        gain = gainv[pl.ds(h * 8, 8), :]
        squares, inner = [], []
        for i in range(B):
            t = b * B + i
            y = Y[t, h] + jnp.sum(z, axis=0)
            if i + 1 < B:
                z = a * z
            Y[t, h] = y
            s = RS[t, h] + F0[t, h] * y
            RS[t, h] = s
            squares.append(s * s)
            inner.append(CT[t, h] * gain * s)
            if h > 0:
                squares[i] = squares[i] + G[t, 0]
                inner[i] = inner[i] + GS[t, 0]
            if h < H - 1:
                G[t, 0] = squares[i]
                GS[t, 0] = inner[i]
        if h == H - 1:
            now = jnp.where(lane == b, column(squares), sums[...])
            sums[...] = jnp.where(lane == nb + b, column(inner), now)
        return later

    for h in range(H):
        arrived(X0.at[pl.ds(h * M, M)], 1 + h)
        lax.fori_loop(0, nb, functools.partial(forward, h), X0[pl.ds(h * M, M)])
    for i in range(1, ntp):
        p = lax.rem(mt + i, ntp)
        pltpu.make_async_remote_copy(
            src_ref=sums, dst_ref=tpr.at[mt], send_sem=ssem.at[10], recv_sem=rsem.at[12],
            device_id=(me, p), device_id_type=MESH,
        ).start()
    pltpu.make_async_copy(sums, tpr.at[mt], rsem.at[12]).start()
    loop(H, weighted)
    arrived(tpr, 12)
    tot = total(tpr[i] for i in range(ntp))
    inner_sum = pltpu.roll(tot, 128 - nb, 1)
    valid = lane < nb
    inv_all = lax.rsqrt(jnp.where(valid, tot, 1.0) / D + 1e-5)
    coef_all = inv_all * inv_all * inv_all * jnp.where(valid, inner_sum, 0.0) / D

    def spread_rows(b):
        at = pl.ds(b * B, B)
        for src, dst in ((inv_all, INVT), (coef_all, CFT)):
            col = jnp.sum(jnp.where(lane == b, src, 0.0), axis=1, keepdims=True)
            full = jnp.broadcast_to(col, (B, 128))
            dst[at] = jnp.broadcast_to(full[:, None, :], (B, 8, 128))

    loop(nb, spread_rows)

    def backward(h):
        a = AP[h, 1]

        def step(i, run):
            b = nb - 1 - i
            at = pl.ds(b * B, B)
            gain = gainv[pl.ds(h * 8, 8), :][None]
            gs = INVT[at] * (CT[at, h] * gain) - RS[at, h] * CFT[at]
            GS[at, h] = gs
            dz = gs * F0[at, h]
            DZ[at, h] = dz
            v = a * dz[B - 1][None] + dz[B - 2][None]
            for s in range(B - 3, -1, -1):
                v = a * v + dz[s][None]
            AB[h, b] = v
            return AP[h, B] * run + v

        S2[pl.ds(h * M, M)] = lax.fori_loop(0, nb, step, jnp.zeros((M, 8, 128), f32))

    for h in range(H):
        backward(h)
        scatter_half(S2, R2, k1, (2, 3), h)

    def store(slot, b, h, value):
        nat[slot][pl.ds(pl.multiple_of(b * 16, 16), 16), pl.ds(h * 1024, 1024)] = value.reshape(
            B, 1024
        ).astype(bf16)

    for h in range(H):

        def early(b, acc):
            at = pl.ds(b * B, B)
            GF0[at, h] = GS[at, h] * Y[at, h]
            return acc + jnp.sum(CT[at, h] * (RS[at, h] * INVT[at]), axis=0)

        T1[50 + h] = lax.fori_loop(0, nb, early, jnp.zeros((8, 128), f32))

    def grad_halo(i, ref):
        return pltpu.make_async_remote_copy(
            src_ref=ref.at[pl.ds(0, HALO)], dst_ref=ref.at[pl.ds(rows, HALO)],
            send_sem=hssem.at[3 + i], recv_sem=hrsem.at[3 + i],
            device_id=peer(lax.rem(me + n - 1, n)), device_id_type=MESH,
        )

    grad_copies = [grad_halo(i, ref) for i, ref in enumerate((GF0, GF1, GF2))]

    @pl.when(me > 0)
    def _():
        grad_copies[0].start()

    def correlate(h):
        def step(b, acc):
            u = [U[b * B + t, h] for t in range(B)]
            dz = [DZ[b * B + t, h] for t in range(B)]
            return tuple(
                acc[k] + total(dz[t] * u[t - k] for t in range(k, B)) for k in range(B)
            )

        zero = jnp.zeros((8, 128), f32)
        out = lax.fori_loop(0, nb, step, (zero,) * B)
        for k in range(B):
            CK[h, k] = out[k]

    loop(H, correlate)
    def inside_back(h):
        def step(b):
            dz = [DZ[b * B + t, h] for t in range(B)]
            kt = [KT[h, k] for k in range(B)]
            for s in range(B):
                G[b * B + s, h] = total(kt[k] * dz[s + k] for k in range(B - s))

        loop(nb, step)

    loop(H, inside_back)
    relay(R2, E2, A0, (2, 3), True, 0)
    relay(R2, E2, A0, (2, 3), True, 1)

    def mode_sums(h):
        def step(b):
            dz = DZ[pl.ds(b * B, B), h]
            x = XB[h, b]
            QA[h] = QA[h] + x * AB[h, b]
            q = total_in_order([WP[h, s] * dz[s][None] for s in range(1, B)])
            SA[h] = SA[h] + x * q

        QA[h] = jnp.zeros((M, 8, 128), f32)
        SA[h] = jnp.zeros((M, 8, 128), f32)
        loop(nb, step)
        a = AP[h, 1]
        gr = a * QA[h]
        gl = a * SA[h]
        for k in range(B):
            c = CK[h, k][None]
            gr = gr + AP[h, k] * c
            gl = gl + WP[h, k] * c
        T1[pl.ds(h * M, M)] = gr
        SA[h] = gl
        T1[48 + h] = CK[h, 0]

    loop(H, mode_sums)

    def filter_sums(h, src, gf, dst, base):
        def step(b, acc):
            win = window(src, b, h)
            g = gf[pl.ds(b * 8, 8), h]
            return tuple(
                acc[j] + jnp.sum(g * win[HALO - j : HALO - j + 8], axis=0) for j in range(KS)
            )

        zero = jnp.zeros((8, 128), f32)
        out = lax.fori_loop(0, rows // 8, step, (zero,) * KS)
        for j in range(KS):
            dst[base + j] = out[j]
        dst[base + KS] = zero

    for h in range(H):
        filter_sums(h, QX, GF0, T1, 32 + h * 8)
    T1[pl.ds(48 + 2 + H, 16 - 2 - H)] = jnp.zeros((16 - 2 - H, 8, 128), f32)
    scatter(T1, RR1, k2, (4, 6))

    @pl.when(me == n - 1)
    def _():
        for ref in (GF0, GF1, GF2):
            ref[pl.ds(rows, 8)] = jnp.zeros((8, H, 8, 128), f32)

    @pl.when(me < n - 1)
    def _():
        grad_copies[0].wait_recv()

    def back_filter(gf, i, slot):
        for h in range(H):

            def step(b):
                win = gf[pl.ds(b * B, B + HALO), h]
                store(slot, b, h, total(SW[i, h, j][None] * win[j : j + B] for j in range(KS)))

            loop(nb, step)

    back_filter(GF0, 0, 1)

    def mixed(h, b, x):
        a = AP[h, 1]
        earlier = AP[h, B] * x + AB[h, b]
        SA[h] = SA[h] + x * PB[h, b]
        z = RA[h] * x
        for i in range(B):
            t = b * B + (B - 1 - i)
            g = G[t, h] + jnp.sum(z, axis=0)
            if i + 1 < B:
                z = a * z
            GF1[t, h] = g * F2[t, h]
            GF2[t, h] = g * F1[t, h]
        return earlier

    reduced = []
    for h in range(H):
        arrived(A0.at[pl.ds(h * M, M)], 4 + h)
        lax.fori_loop(
            0, nb, lambda i, x: mixed(h, nb - 1 - i, x), A0[pl.ds(h * M, M)]
        )
        if h == H - 1:

            @pl.when(me > 0)
            def _():
                grad_copies[1].start()
                grad_copies[2].start()

        mine = T2.at[h]
        mine[pl.ds(0, M)] = -RT[h] * SA[h]
        filter_sums(h, KX, GF1, mine, 16)
        filter_sums(h, VX, GF2, mine, 24)
        scatter(mine, RR2.at[h], k3, (6 + h, 8 + h))

    def reduce(src, dst, size):
        dst[...] = total(src[pl.ds(i * size, size)] for i in range(n))

    arrived(RR1, 6)
    reduce(RR1, SUM1, k2)
    spread(SUM1, AG1, k2, (5, 7))

    @pl.when(me < n - 1)
    def _():
        grad_copies[1].wait_recv()
        grad_copies[2].wait_recv()

    back_filter(GF1, 1, 2)
    arrived(RR2.at[0], 8)
    reduce(RR2.at[0], SUM2.at[0], k3)
    spread(SUM2.at[0], AG2.at[0], k3, (8, 10))
    back_filter(GF2, 2, 3)
    for h in range(1, H):
        arrived(RR2.at[h], 8 + h)
        reduce(RR2.at[h], SUM2.at[h], k3)
        spread(SUM2.at[h], AG2.at[h], k3, (8 + h, 10 + h))

    for h in range(H):

        def late(b):
            at = pl.ds(b * B, B)
            gain = gainv[pl.ds(h * 8, 8), :][None]
            store(0, b, h, RS[at, h] * INVT[at] * gain)
            store(4, b, h, GS[at, h])

        loop(nb, late)

    def natural(src, at, count):
        return src[pl.ds(at, count)].reshape(count, 1024)

    arrived(AG1, 7)
    for h in range(H):
        cols = pl.ds(h * 1024, 1024)
        gr_o[:, cols] = natural(AG1, h * M, M)
        short_o[0, :, cols] = natural(AG1, 32 + h * 8, 8)[0:KS]
        gskip_o[pl.ds(h * 8, 8), :] = AG1[48 + h]
        ggain_o[pl.ds(h * 8, 8), :] = AG1[50 + h]
    for h in range(H):
        cols = pl.ds(h * 1024, 1024)
        arrived(AG2.at[h], 10 + h)
        gl_o[:, cols] = natural(AG2.at[h], 0, M)
        short_o[1, :, cols] = natural(AG2.at[h], 16, 8)[0:KS]
        short_o[2, :, cols] = natural(AG2.at[h], 24, 8)[0:KS]

    for at, dst, size in (
        (0, R1, k1), (1, X0, k1), (2, R2, k1), (3, A0, k1), (4, RR1, k2), (5, AG1, k2),
        (6, RR2.at[0], k3), (7, RR2.at[1], k3), (8, AG2.at[0], k3), (9, AG2.at[1], k3),
    ):
        sent(dst, size, at)
    others = tpr.at[pl.ds(0, ntp - 1)]
    pltpu.make_async_copy(others, others, ssem.at[10]).wait()

    @pl.when(me < n - 1)
    def _():
        for copy in halo_copies:
            copy.wait_send()

    @pl.when(me > 0)
    def _():
        for copy in grad_copies:
            copy.wait_send()


def deliver(*refs):
    ins, outs, sem = refs[:10], refs[10:20], refs[20]
    copies = [pltpu.make_async_copy(s, d, sem.at[i]) for i, (s, d) in enumerate(zip(ins, outs))]
    for copy in copies:
        copy.start()
    for copy in copies:
        copy.wait()


def shards(
    n, ntp, residual, query_in, key_in, value_in, short_filter, residues, decay_rate, skip_gain,
    norm_gain, cotangent,
):
    rows, width = residual.shape
    H = width // 1024
    nb = rows // B
    tiles = H * M

    def V(*shape, dtype=f32):
        return pltpu.VMEM(shape, dtype)

    def tm(extra=0):
        return V(rows + extra, H, 8, 128)

    def tile(count):
        return V(count, 8, 128)

    k2, k3 = 64 // n, 32 // n
    scratch = (
        [V(3, 16, width, dtype=bf16)]
        + [V(3, KS, width), V(M, width), V(M, width), V(H * 8, 128), V(H * 8, 128)]
        + [tm(8)] * 3 + [tm()] * 10 + [tm(8)] * 3
        + [V(H, B + 1, M, 8, 128)] * 2
        + [V(H, B + 1, 8, 128), V(H, M, 8, 128), V(H, M, 8, 128), V(3, H, 8, 8, 128), tile(tiles)]
        + [V(H, nb, M, 8, 128)] * 3
        + [tile(tiles)] * 8
        + [V(B, 128), V(ntp, B, 128), tile(rows), tile(rows)]
        + [V(H, M, 8, 128)] * 3
        + [V(H, B, 8, 128), V(8, 1024)]
        + [tile(64), tile(64), tile(k2), tile(64)]
        + [V(H, 32, 8, 128), V(H, 32, 8, 128), V(H, k3, 8, 128), V(H, 32, 8, 128)]
        + [pltpu.SemaphoreType.DMA((c,)) for c in (10, 11, 13, 6, 6)]
    )
    big = jax.ShapeDtypeStruct((rows, width), bf16)
    vec = jax.ShapeDtypeStruct((H * 8, 128), f32)
    out_shape = (
        [big] * 5
        + [jax.ShapeDtypeStruct((3, KS, width), f32)]
        + [jax.ShapeDtypeStruct((M, width), f32)] * 2
        + [vec, vec]
    )
    anywhere = pl.BlockSpec(memory_space=pl.ANY)
    outs = pl.pallas_call(
        functools.partial(kernel, n, ntp, rows, width),
        out_shape=[V(*o.shape, dtype=o.dtype) for o in out_shape],
        in_specs=[anywhere] * 10,
        out_specs=[pl.BlockSpec(memory_space=pltpu.VMEM)] * 10,
        scratch_shapes=scratch,
        compiler_params=pltpu.CompilerParams(
            collective_id=0, has_side_effects=True, vmem_limit_bytes=52 << 20
        ),
    )(
        residual, query_in, key_in, value_in, short_filter, residues, decay_rate,
        skip_gain.reshape(H * 8, 128), norm_gain.reshape(H * 8, 128), cotangent,
    )
    outs = pl.pallas_call(
        deliver,
        out_shape=out_shape,
        in_specs=[anywhere] * 10,
        out_specs=[anywhere] * 10,
        scratch_shapes=[pltpu.SemaphoreType.DMA((10,))],
        compiler_params=pltpu.CompilerParams(vmem_limit_bytes=1 << 20),
    )(*outs)
    return (*outs[:8], outs[8].reshape(width), outs[9].reshape(width))


def solution(mesh):
    act, par, vec = P("ctx", "tp"), P(None, "tp"), P("tp")
    short = P(None, None, "tp")
    return jax.shard_map(
        functools.partial(shards, mesh.shape["ctx"], mesh.shape["tp"]),
        mesh=mesh,
        in_specs=(act, act, act, act, short, par, par, vec, vec, act),
        out_specs=(act, act, act, act, act, short, par, par, vec, vec),
        check_vma=False,
    )
```

time: 80.5 us -> 70.5 us (0.88)
  Pallas kernels: 79.7 us -> 69.7 us
    pallas_call x1, Pallas kernels: 77.2 us -> 67.2 us  [shards(): pl.pallas_call(functools.partial(kernel, n, ntp, rows, width), out_shape=...]
where the time goes in v3:
time: 70.5 us; the launch traced here: 70.4 us
  Pallas kernels  69.7 us (99%)
    pallas_call x1, Pallas kernels, shards(): pl.pallas_call(functools.partial(kernel, n, ntp, rows, width), out_shape=...  67.2 us
    pallas_call x1, Pallas kernels, shards(): pl.pallas_call(deliver, out_shape=out_shape, in_specs=[anywhere] * 10, ou...  2.55 us

profile of v3, /device:TPU:1, one launch (start us, length us, event | category | flops | bytes accessed | tf_op | source)
XLA Modules:
  0.0 70.4 jit_solution(14992140349433714748)
XLA Ops:
  0.6 67.2 %shard_map.177 = (bf16[256,2048]{1,0:T(8,128)(2,1)S(1)}, bf16[256,2048]{1,0:T(8,128)(2,1)S(1)}, bf16[256,2048]{1,0:T(8,128)(2,1)S(1)}, bf16[256,2048]{1,0:T(8,12...) custom-call(bf16[256,2048]{1,0:T(8,128)(2,1)} %res_h.1, ...), custom_call_target="tpu_custom_call" | custom-call | tf_op jit(solution)/shard_map/pallas_call | solution.py:655
  67.8 2.5 %shard_map.178 = (bf16[256,2048]{1,0:T(8,128)(2,1)}, bf16[256,2048]{1,0:T(8,128)(2,1)}, bf16[256,2048]{1,0:T(8,128)(2,1)}, bf16[256,2048]{1,0:T(8,128)(2,1)}, bf...) custom-call(bf16[256,2048]{1,0:T(8,128)(2,1)S(1)} %get-tuple-element, ...), custom_call_target="tpu_custom_call" | custom-call | tf_op jit(solution)/shard_map/pallas_call | solution.py:668

commit v4 on v3

--- a/solution.py
+++ b/solution.py
@@ -42,7 +42,7 @@
     QX, KX, VX, RS, CT, F0, F1, F2, U, Y, DZ, GS, G, GF0, GF1, GF2,
     AP, WP, KT, RT, LM, SW, AT, XB, PB, AB,
     S1, R1, E1, X0, S2, R2, E2, A0,
-    sums, tpr, INVT, CFT, RA, SA, QA, CK, SG,
+    sums, tpr, NS, INVR, CFR, RA, SA, QA, CK, SG,
     T1, RR1, SUM1, AG1, T2, RR2, SUM2, AG2,
     insem, ssem, rsem, hssem, hrsem,
 ):
@@ -110,12 +110,12 @@
 
     def in_halo(i, src):
         return pltpu.make_async_remote_copy(
-            src_ref=src.at[pl.ds(rows - 16, 16)], dst_ref=halo.at[i],
+            src_ref=src.at[pl.ds(rows - 8, 8)], dst_ref=halo.at[i],
             send_sem=hssem.at[i], recv_sem=hrsem.at[i],
             device_id=peer(lax.rem(me + 1, n)), device_id_type=MESH,
         )
 
-    halo_copies = [in_halo(0, q_h), in_halo(1, k_h), in_halo(2, v_h)]
+    halo_copies = [in_halo(0, q_h), in_halo(1, nat[2]), in_halo(2, nat[3])]
 
     @pl.when(me < n - 1)
     def _():
@@ -151,21 +151,24 @@
 
         S1[pl.ds(h * M, M)] = lax.fori_loop(1, nb, step, jnp.zeros((M, 8, 128), f32))
 
-    for h in range(H):
+    loop(rows // 8, functools.partial(feature, 0), 1)
+    summary(0)
+    for h in range(1, H):
         loop(rows // 8, functools.partial(feature, h), 1)
-    loop(H, summary)
-
-    @pl.when(me > 0)
-    def _():
-        for i in (1, 2, 0):
+
+    def first_rows(i, dst):
+        @pl.when(me > 0)
+        def _():
             halo_copies[i].wait_recv()
 
-    @pl.when(me == 0)
-    def _():
-        halo[...] = jnp.zeros(halo.shape, bf16)
-
-    for i, dst in enumerate((QX, KX, VX)):
-        dst[pl.ds(0, 8)] = halo[i].astype(f32)[8:16].reshape(8, H, 8, 128)
+        @pl.when(me == 0)
+        def _():
+            halo[i] = jnp.zeros(halo.shape[1:], bf16)
+
+        dst[pl.ds(0, 8)] = halo[i].astype(f32).reshape(8, H, 8, 128)
+
+    first_rows(1, KX)
+    first_rows(2, VX)
 
     half = n // H
 
@@ -180,16 +183,20 @@
 
     def scatter(src, dst, size, at):
         mine = part(dst, me, size)
-        for i in range(1, n):
+        def step(i):
             p = lax.rem(me + i, n)
             remote(part(src, p, size), mine, p, at)
+
+        loop(n, step, 1)
         pltpu.make_async_copy(part(src, me, size), mine, rsem.at[at[1]]).start()
 
     def scatter_half(src, dst, size, at, h):
         mine = part(dst, me, size)
-        for i in range(1, half):
+        def step(i):
             p = h * half + lax.rem(me + i, half)
             remote(part(src, p, size), mine, p, at)
+
+        loop(half, step, 1)
         first = me < half if h == 0 else me >= half
         other = me >= half if h == 0 else me < half
 
@@ -204,8 +211,7 @@
 
     def spread(src, dst, size, at):
         mine = part(dst, me, size)
-        for i in range(1, n):
-            remote(src, mine, lax.rem(me + i, n), at)
+        loop(n, lambda i: remote(src, mine, lax.rem(me + i, n), at), 1)
         pltpu.make_async_copy(src, mine, rsem.at[at[1]]).start()
 
     def arrived(dst, at):
@@ -232,6 +238,8 @@
             scatter(mid, dst, k1, (at[0] + 1, at[1] + 1 + h))
 
     for h in range(H):
+        if h > 0:
+            summary(h)
         feature(h, 0)
         S1[pl.ds(h * M, M)] = S1[pl.ds(h * M, M)] + gather(h, 0) * jnp.exp(
             LM[h] * (-float(rows - B))
@@ -266,6 +274,7 @@
     loop(H, inside)
     in_copies[7].wait()
     to_tm(1, QX, 8)
+    first_rows(0, QX)
     relay(R1, E1, X0, (0, 0), False, 0)
     relay(R1, E1, X0, (0, 0), False, 1)
 
@@ -279,7 +288,13 @@
     in_copies[8].wait()
     to_tm(0, RS, 0)
     in_copies[9].wait()
-    to_tm(4, CT, 0)
+    gain_tm = gainv[...].reshape(1, H, 8, 128)
+
+    def to_gain_term(i):
+        v = nat[4][pl.ds(pl.multiple_of(i * 16, 16), 16), :].astype(f32)
+        CT[pl.ds(i * 16, 16)] = v.reshape(16, H, 8, 128) * gain_tm
+
+    loop(rows // 16, to_gain_term)
 
     def total_in_order(terms):
         out = terms[0]
@@ -298,18 +313,18 @@
 
         loop(nb, step)
 
-    lane = lax.broadcasted_iota(jnp.int32, (B, 128), 1)
-    sums[...] = jnp.zeros((B, 128), f32)
-
-    def column(parts):
-        return jnp.sum(jnp.stack(parts).reshape(B, 1024), axis=1, keepdims=True)
+    groups = rows // 8
+    lane = lax.broadcasted_iota(jnp.int32, (8, 128), 1)
+
+    def fold(parts):
+        flat = jnp.stack(parts).reshape(8, 1024)
+        return total(flat[:, i * 128 : (i + 1) * 128] for i in range(8))
 
     def forward(h, b, x):
         a = AP[h, 1]
         z = RA[h] * x
         later = AP[h, B] * x + XB[h, b]
         XB[h, b] = x
-        gain = gainv[pl.ds(h * 8, 8), :]
         squares, inner = [], []
         for i in range(B):
             t = b * B + i
@@ -320,21 +335,27 @@
             s = RS[t, h] + F0[t, h] * y
             RS[t, h] = s
             squares.append(s * s)
-            inner.append(CT[t, h] * gain * s)
+            inner.append(CT[t, h] * s)
             if h > 0:
                 squares[i] = squares[i] + G[t, 0]
                 inner[i] = inner[i] + GS[t, 0]
             if h < H - 1:
                 G[t, 0] = squares[i]
                 GS[t, 0] = inner[i]
-        if h == H - 1:
-            now = jnp.where(lane == b, column(squares), sums[...])
-            sums[...] = jnp.where(lane == nb + b, column(inner), now)
+            if h == H - 1 and i % 8 == 7:
+                NS[0, b * 2 + i // 8] = fold(squares[i - 7 : i + 1])
+                NS[1, b * 2 + i // 8] = fold(inner[i - 7 : i + 1])
         return later
 
     for h in range(H):
         arrived(X0.at[pl.ds(h * M, M)], 1 + h)
         lax.fori_loop(0, nb, functools.partial(forward, h), X0[pl.ds(h * M, M)])
+    gathered = jnp.zeros((8, 128), f32)
+    for q in range(2):
+        for g in range(groups):
+            col = jnp.sum(NS[q, g], axis=1, keepdims=True)
+            gathered = jnp.where(lane == q * groups + g, col, gathered)
+    sums[...] = gathered
     for i in range(1, ntp):
         p = lax.rem(mt + i, ntp)
         pltpu.make_async_remote_copy(
@@ -345,19 +366,18 @@
     loop(H, weighted)
     arrived(tpr, 12)
     tot = total(tpr[i] for i in range(ntp))
-    inner_sum = pltpu.roll(tot, 128 - nb, 1)
-    valid = lane < nb
+    inner_sum = pltpu.roll(tot, 128 - groups, 1)
+    valid = lane < groups
     inv_all = lax.rsqrt(jnp.where(valid, tot, 1.0) / D + 1e-5)
     coef_all = inv_all * inv_all * inv_all * jnp.where(valid, inner_sum, 0.0) / D
 
-    def spread_rows(b):
-        at = pl.ds(b * B, B)
-        for src, dst in ((inv_all, INVT), (coef_all, CFT)):
-            col = jnp.sum(jnp.where(lane == b, src, 0.0), axis=1, keepdims=True)
-            full = jnp.broadcast_to(col, (B, 128))
-            dst[at] = jnp.broadcast_to(full[:, None, :], (B, 8, 128))
-
-    loop(nb, spread_rows)
+    for g in range(groups):
+        at = pl.ds(g * 8, 8)
+        INVR[at, :] = jnp.broadcast_to(inv_all[:, g : g + 1], (8, 128))
+        CFR[at, :] = jnp.broadcast_to(coef_all[:, g : g + 1], (8, 128))
+
+    def row(ref, t):
+        return jnp.broadcast_to(ref[pl.ds(t, 1), :], (8, 128))
 
     def backward(h):
         a = AP[h, 1]
@@ -365,8 +385,9 @@
         def step(i, run):
             b = nb - 1 - i
             at = pl.ds(b * B, B)
-            gain = gainv[pl.ds(h * 8, 8), :][None]
-            gs = INVT[at] * (CT[at, h] * gain) - RS[at, h] * CFT[at]
+            inv = jnp.stack([row(INVR, b * B + t) for t in range(B)])
+            coef = jnp.stack([row(CFR, b * B + t) for t in range(B)])
+            gs = inv * CT[at, h] - RS[at, h] * coef
             GS[at, h] = gs
             dz = gs * F0[at, h]
             DZ[at, h] = dz
@@ -392,9 +413,11 @@
         def early(b, acc):
             at = pl.ds(b * B, B)
             GF0[at, h] = GS[at, h] * Y[at, h]
-            return acc + jnp.sum(CT[at, h] * (RS[at, h] * INVT[at]), axis=0)
-
-        T1[50 + h] = lax.fori_loop(0, nb, early, jnp.zeros((8, 128), f32))
+            inv = jnp.stack([row(INVR, b * B + t) for t in range(B)])
+            return acc + jnp.sum(CT[at, h] * (RS[at, h] * inv), axis=0)
+
+        acc = lax.fori_loop(0, nb, early, jnp.zeros((8, 128), f32))
+        T1[50 + h] = acc / gainv[pl.ds(h * 8, 8), :]
 
     def grad_halo(i, ref):
         return pltpu.make_async_remote_copy(
@@ -423,6 +446,25 @@
             CK[h, k] = out[k]
 
     loop(H, correlate)
+
+    def filter_sums(h, src, gf, dst, base):
+        def step(b, acc):
+            win = window(src, b, h)
+            g = gf[pl.ds(b * 8, 8), h]
+            return tuple(
+                acc[j] + jnp.sum(g * win[HALO - j : HALO - j + 8], axis=0) for j in range(KS)
+            )
+
+        zero = jnp.zeros((8, 128), f32)
+        out = lax.fori_loop(0, rows // 8, step, (zero,) * KS)
+        for j in range(KS):
+            dst[base + j] = out[j]
+        dst[base + KS] = zero
+
+    for h in range(H):
+        filter_sums(h, QX, GF0, T1, 32 + h * 8)
+    T1[pl.ds(48 + 2 + H, 16 - 2 - H)] = jnp.zeros((16 - 2 - H, 8, 128), f32)
+
     def inside_back(h):
         def step(b):
             dz = [DZ[b * B + t, h] for t in range(B)]
@@ -432,9 +474,6 @@
 
         loop(nb, step)
 
-    loop(H, inside_back)
-    relay(R2, E2, A0, (2, 3), True, 0)
-    relay(R2, E2, A0, (2, 3), True, 1)
 
     def mode_sums(h):
         def step(b):
@@ -458,26 +497,11 @@
         SA[h] = gl
         T1[48 + h] = CK[h, 0]
 
-    loop(H, mode_sums)
-
-    def filter_sums(h, src, gf, dst, base):
-        def step(b, acc):
-            win = window(src, b, h)
-            g = gf[pl.ds(b * 8, 8), h]
-            return tuple(
-                acc[j] + jnp.sum(g * win[HALO - j : HALO - j + 8], axis=0) for j in range(KS)
-            )
-
-        zero = jnp.zeros((8, 128), f32)
-        out = lax.fori_loop(0, rows // 8, step, (zero,) * KS)
-        for j in range(KS):
-            dst[base + j] = out[j]
-        dst[base + KS] = zero
-
-    for h in range(H):
-        filter_sums(h, QX, GF0, T1, 32 + h * 8)
-    T1[pl.ds(48 + 2 + H, 16 - 2 - H)] = jnp.zeros((16 - 2 - H, 8, 128), f32)
-    scatter(T1, RR1, k2, (4, 6))
+    mode_sums(0)
+    relay(R2, E2, A0, (2, 3), True, 0)
+    loop(H, mode_sums, 1)
+    relay(R2, E2, A0, (2, 3), True, 1)
+    loop(H, inside_back)
 
     @pl.when(me == n - 1)
     def _():
@@ -496,6 +520,11 @@
                 store(slot, b, h, total(SW[i, h, j][None] * win[j : j + B] for j in range(KS)))
 
             loop(nb, step)
+
+    @pl.when(me < n - 1)
+    def _():
+        for copy in halo_copies:
+            copy.wait_send()
 
     back_filter(GF0, 0, 1)
 
@@ -513,9 +542,13 @@
             GF2[t, h] = g * F1[t, h]
         return earlier
 
-    reduced = []
+    def reduce(src, dst, size):
+        dst[...] = total(src[pl.ds(i * size, size)] for i in range(n))
+
     for h in range(H):
         arrived(A0.at[pl.ds(h * M, M)], 4 + h)
+        if h == 0:
+            scatter(T1, RR1, k2, (4, 6))
         lax.fori_loop(
             0, nb, lambda i, x: mixed(h, nb - 1 - i, x), A0[pl.ds(h * M, M)]
         )
@@ -532,19 +565,15 @@
         filter_sums(h, VX, GF2, mine, 24)
         scatter(mine, RR2.at[h], k3, (6 + h, 8 + h))
 
-    def reduce(src, dst, size):
-        dst[...] = total(src[pl.ds(i * size, size)] for i in range(n))
-
-    arrived(RR1, 6)
-    reduce(RR1, SUM1, k2)
-    spread(SUM1, AG1, k2, (5, 7))
-
     @pl.when(me < n - 1)
     def _():
         grad_copies[1].wait_recv()
         grad_copies[2].wait_recv()
 
     back_filter(GF1, 1, 2)
+    arrived(RR1, 6)
+    reduce(RR1, SUM1, k2)
+    spread(SUM1, AG1, k2, (5, 7))
     arrived(RR2.at[0], 8)
     reduce(RR2.at[0], SUM2.at[0], k3)
     spread(SUM2.at[0], AG2.at[0], k3, (8, 10))
@@ -559,7 +588,8 @@
         def late(b):
             at = pl.ds(b * B, B)
             gain = gainv[pl.ds(h * 8, 8), :][None]
-            store(0, b, h, RS[at, h] * INVT[at] * gain)
+            inv = jnp.stack([row(INVR, b * B + t) for t in range(B)])
+            store(0, b, h, RS[at, h] * inv * gain)
             store(4, b, h, GS[at, h])
 
         loop(nb, late)
@@ -588,11 +618,6 @@
         sent(dst, size, at)
     others = tpr.at[pl.ds(0, ntp - 1)]
     pltpu.make_async_copy(others, others, ssem.at[10]).wait()
-
-    @pl.when(me < n - 1)
-    def _():
-        for copy in halo_copies:
-            copy.wait_send()
 
     @pl.when(me > 0)
     def _():
@@ -629,14 +654,14 @@
 
     k2, k3 = 64 // n, 32 // n
     scratch = (
-        [V(3, 16, width, dtype=bf16)]
+        [V(3, 8, width, dtype=bf16)]
         + [V(3, KS, width), V(M, width), V(M, width), V(H * 8, 128), V(H * 8, 128)]
         + [tm(8)] * 3 + [tm()] * 10 + [tm(8)] * 3
         + [V(H, B + 1, M, 8, 128)] * 2
         + [V(H, B + 1, 8, 128), V(H, M, 8, 128), V(H, M, 8, 128), V(3, H, 8, 8, 128), tile(tiles)]
         + [V(H, nb, M, 8, 128)] * 3
         + [tile(tiles)] * 8
-        + [V(B, 128), V(ntp, B, 128), tile(rows), tile(rows)]
+        + [V(8, 128), tile(ntp), V(2, rows // 8, 8, 128), V(rows, 128), V(rows, 128)]
         + [V(H, M, 8, 128)] * 3
         + [V(H, B, 8, 128), V(8, 1024)]
         + [tile(64), tile(64), tile(k2), tile(64)]

time: 70.5 us -> 67.2 us (0.953)
  Pallas kernels: 69.7 us -> 66.5 us
    pallas_call x1, Pallas kernels: 67.2 us -> 63.9 us  [shards(): pl.pallas_call(functools.partial(kernel, n, ntp, rows, width), out_shape=...]
where the time goes in v4:
time: 67.2 us; the launch traced here: 67.1 us
  Pallas kernels  66.5 us (99%)
    pallas_call x1, Pallas kernels, shards(): pl.pallas_call(functools.partial(kernel, n, ntp, rows, width), out_shape=...  63.9 us
    pallas_call x1, Pallas kernels, shards(): pl.pallas_call(deliver, out_shape=out_shape, in_specs=[anywhere] * 10, ou...  2.55 us

profile of v4, /device:TPU:1, one launch (start us, length us, event | category | flops | bytes accessed | tf_op | source)
XLA Modules:
  0.0 67.1 jit_solution(8036072958351219603)
XLA Ops:
  0.6 63.9 %shard_map.177 = (bf16[256,2048]{1,0:T(8,128)(2,1)S(1)}, bf16[256,2048]{1,0:T(8,128)(2,1)S(1)}, bf16[256,2048]{1,0:T(8,128)(2,1)S(1)}, bf16[256,2048]{1,0:T(8,12...) custom-call(bf16[256,2048]{1,0:T(8,128)(2,1)} %res_h.1, ...), custom_call_target="tpu_custom_call" | custom-call | tf_op jit(solution)/shard_map/pallas_call | solution.py:680
  64.6 2.5 %shard_map.178 = (bf16[256,2048]{1,0:T(8,128)(2,1)}, bf16[256,2048]{1,0:T(8,128)(2,1)}, bf16[256,2048]{1,0:T(8,128)(2,1)}, bf16[256,2048]{1,0:T(8,128)(2,1)}, bf...) custom-call(bf16[256,2048]{1,0:T(8,128)(2,1)S(1)} %get-tuple-element, ...), custom_call_target="tpu_custom_call" | custom-call | tf_op jit(solution)/shard_map/pallas_call | solution.py:693

commit v5 on v4

--- a/solution.py
+++ b/solution.py
@@ -43,7 +43,7 @@
     AP, WP, KT, RT, LM, SW, AT, XB, PB, AB,
     S1, R1, E1, X0, S2, R2, E2, A0,
     sums, tpr, NS, INVR, CFR, RA, SA, QA, CK, SG,
-    T1, RR1, SUM1, AG1, T2, RR2, SUM2, AG2,
+    T1, RR1, SUM1, AG1, T1A, RR1A, SUM1A, AG1A, T2, RR2, SUM2, AG2,
     insem, ssem, rsem, hssem, hrsem,
 ):
     H = width // 1024
@@ -53,7 +53,6 @@
     mt = lax.axis_index("tp")
     tiles = H * M
     k1 = tiles // n
-    k2 = 64 // n
     k3 = 32 // n
 
     def peer(p):
@@ -417,7 +416,7 @@
             return acc + jnp.sum(CT[at, h] * (RS[at, h] * inv), axis=0)
 
         acc = lax.fori_loop(0, nb, early, jnp.zeros((8, 128), f32))
-        T1[50 + h] = acc / gainv[pl.ds(h * 8, 8), :]
+        T1A[18 + h] = acc / gainv[pl.ds(h * 8, 8), :]
 
     def grad_halo(i, ref):
         return pltpu.make_async_remote_copy(
@@ -462,8 +461,10 @@
         dst[base + KS] = zero
 
     for h in range(H):
-        filter_sums(h, QX, GF0, T1, 32 + h * 8)
-    T1[pl.ds(48 + 2 + H, 16 - 2 - H)] = jnp.zeros((16 - 2 - H, 8, 128), f32)
+        filter_sums(h, QX, GF0, T1A, h * 8)
+        T1A[16 + h] = CK[h, 0]
+    T1A[pl.ds(18 + H, 14 - H)] = jnp.zeros((14 - H, 8, 128), f32)
+    scatter(T1A, RR1A, k3, (11, 13))
 
     def inside_back(h):
         def step(b):
@@ -495,7 +496,6 @@
             gl = gl + WP[h, k] * c
         T1[pl.ds(h * M, M)] = gr
         SA[h] = gl
-        T1[48 + h] = CK[h, 0]
 
     mode_sums(0)
     relay(R2, E2, A0, (2, 3), True, 0)
@@ -521,12 +521,6 @@
 
             loop(nb, step)
 
-    @pl.when(me < n - 1)
-    def _():
-        for copy in halo_copies:
-            copy.wait_send()
-
-    back_filter(GF0, 0, 1)
 
     def mixed(h, b, x):
         a = AP[h, 1]
@@ -548,7 +542,7 @@
     for h in range(H):
         arrived(A0.at[pl.ds(h * M, M)], 4 + h)
         if h == 0:
-            scatter(T1, RR1, k2, (4, 6))
+            scatter(T1, RR1, k3, (4, 6))
         lax.fori_loop(
             0, nb, lambda i, x: mixed(h, nb - 1 - i, x), A0[pl.ds(h * M, M)]
         )
@@ -559,6 +553,10 @@
                 grad_copies[1].start()
                 grad_copies[2].start()
 
+        if h == 0:
+            arrived(RR1A, 13)
+            reduce(RR1A, SUM1A, k3)
+            spread(SUM1A, AG1A, k3, (12, 14))
         mine = T2.at[h]
         mine[pl.ds(0, M)] = -RT[h] * SA[h]
         filter_sums(h, KX, GF1, mine, 16)
@@ -567,21 +565,18 @@
 
     @pl.when(me < n - 1)
     def _():
-        grad_copies[1].wait_recv()
-        grad_copies[2].wait_recv()
-
-    back_filter(GF1, 1, 2)
-    arrived(RR1, 6)
-    reduce(RR1, SUM1, k2)
-    spread(SUM1, AG1, k2, (5, 7))
+        for copy in halo_copies:
+            copy.wait_send()
+
+    back_filter(GF0, 0, 1)
+
     arrived(RR2.at[0], 8)
     reduce(RR2.at[0], SUM2.at[0], k3)
     spread(SUM2.at[0], AG2.at[0], k3, (8, 10))
-    back_filter(GF2, 2, 3)
-    for h in range(1, H):
-        arrived(RR2.at[h], 8 + h)
-        reduce(RR2.at[h], SUM2.at[h], k3)
-        spread(SUM2.at[h], AG2.at[h], k3, (8 + h, 10 + h))
+
+    arrived(RR1, 6)
+    reduce(RR1, SUM1, k3)
+    spread(SUM1, AG1, k3, (5, 7))
 
     for h in range(H):
 
@@ -594,16 +589,31 @@
 
         loop(nb, late)
 
+    for h in range(1, H):
+        arrived(RR2.at[h], 8 + h)
+        reduce(RR2.at[h], SUM2.at[h], k3)
+        spread(SUM2.at[h], AG2.at[h], k3, (8 + h, 10 + h))
+
+    @pl.when(me < n - 1)
+    def _():
+        grad_copies[1].wait_recv()
+        grad_copies[2].wait_recv()
+
+    back_filter(GF1, 1, 2)
+
+    back_filter(GF2, 2, 3)
+
     def natural(src, at, count):
         return src[pl.ds(at, count)].reshape(count, 1024)
 
+    arrived(AG1A, 14)
     arrived(AG1, 7)
     for h in range(H):
         cols = pl.ds(h * 1024, 1024)
         gr_o[:, cols] = natural(AG1, h * M, M)
-        short_o[0, :, cols] = natural(AG1, 32 + h * 8, 8)[0:KS]
-        gskip_o[pl.ds(h * 8, 8), :] = AG1[48 + h]
-        ggain_o[pl.ds(h * 8, 8), :] = AG1[50 + h]
+        short_o[0, :, cols] = natural(AG1A, h * 8, 8)[0:KS]
+        gskip_o[pl.ds(h * 8, 8), :] = AG1A[16 + h]
+        ggain_o[pl.ds(h * 8, 8), :] = AG1A[18 + h]
     for h in range(H):
         cols = pl.ds(h * 1024, 1024)
         arrived(AG2.at[h], 10 + h)
@@ -612,7 +622,7 @@
         short_o[2, :, cols] = natural(AG2.at[h], 24, 8)[0:KS]
 
     for at, dst, size in (
-        (0, R1, k1), (1, X0, k1), (2, R2, k1), (3, A0, k1), (4, RR1, k2), (5, AG1, k2),
+        (0, R1, k1), (1, X0, k1), (2, R2, k1), (3, A0, k1), (4, RR1, k3), (5, AG1, k3), (11, RR1A, k3), (12, AG1A, k3),
         (6, RR2.at[0], k3), (7, RR2.at[1], k3), (8, AG2.at[0], k3), (9, AG2.at[1], k3),
     ):
         sent(dst, size, at)
@@ -652,7 +662,7 @@
     def tile(count):
         return V(count, 8, 128)
 
-    k2, k3 = 64 // n, 32 // n
+    k3 = 32 // n
     scratch = (
         [V(3, 8, width, dtype=bf16)]
         + [V(3, KS, width), V(M, width), V(M, width), V(H * 8, 128), V(H * 8, 128)]
@@ -664,9 +674,9 @@
         + [V(8, 128), tile(ntp), V(2, rows // 8, 8, 128), V(rows, 128), V(rows, 128)]
         + [V(H, M, 8, 128)] * 3
         + [V(H, B, 8, 128), V(8, 1024)]
-        + [tile(64), tile(64), tile(k2), tile(64)]
+        + [tile(32), tile(32), tile(k3), tile(32)] * 2
         + [V(H, 32, 8, 128), V(H, 32, 8, 128), V(H, k3, 8, 128), V(H, 32, 8, 128)]
-        + [pltpu.SemaphoreType.DMA((c,)) for c in (10, 11, 13, 6, 6)]
+        + [pltpu.SemaphoreType.DMA((c,)) for c in (10, 13, 15, 6, 6)]
     )
     big = jax.ShapeDtypeStruct((rows, width), bf16)
     vec = jax.ShapeDtypeStruct((H * 8, 128), f32)

time: 67.2 us -> 66.1 us (0.984)
  Pallas kernels: 66.5 us -> 65.4 us
    pallas_call x1, Pallas kernels: 63.9 us -> 62.8 us  [shards(): pl.pallas_call(functools.partial(kernel, n, ntp, rows, width), out_shape=...]
where the time goes in v5:
time: 66.1 us; the launch traced here: 66 us
  Pallas kernels  65.4 us (99%)
    pallas_call x1, Pallas kernels, shards(): pl.pallas_call(functools.partial(kernel, n, ntp, rows, width), out_shape=...  62.8 us
    pallas_call x1, Pallas kernels, shards(): pl.pallas_call(deliver, out_shape=out_shape, in_specs=[anywhere] * 10, ou...  2.55 us

profile of v5, /device:TPU:1, one launch (start us, length us, event | category | flops | bytes accessed | tf_op | source)
XLA Modules:
  0.0 66.0 jit_solution(7322015581911387696)
XLA Ops:
  0.6 62.8 %shard_map.177 = (bf16[256,2048]{1,0:T(8,128)(2,1)S(1)}, bf16[256,2048]{1,0:T(8,128)(2,1)S(1)}, bf16[256,2048]{1,0:T(8,128)(2,1)S(1)}, bf16[256,2048]{1,0:T(8,12...) custom-call(bf16[256,2048]{1,0:T(8,128)(2,1)} %res_h.1, ...), custom_call_target="tpu_custom_call" | custom-call | tf_op jit(solution)/shard_map/pallas_call | solution.py:690
  63.5 2.5 %shard_map.178 = (bf16[256,2048]{1,0:T(8,128)(2,1)}, bf16[256,2048]{1,0:T(8,128)(2,1)}, bf16[256,2048]{1,0:T(8,128)(2,1)}, bf16[256,2048]{1,0:T(8,128)(2,1)}, bf...) custom-call(bf16[256,2048]{1,0:T(8,128)(2,1)S(1)} %get-tuple-element, ...), custom_call_target="tpu_custom_call" | custom-call | tf_op jit(solution)/shard_map/pallas_call | solution.py:703

commit v6 on v5

--- a/solution.py
+++ b/solution.py
@@ -183,7 +183,7 @@
     def scatter(src, dst, size, at):
         mine = part(dst, me, size)
         def step(i):
-            p = lax.rem(me + i, n)
+            p = lax.rem(me + lax.rem(i + n // 2 - 2, n - 1) + 1, n)
             remote(part(src, p, size), mine, p, at)
 
         loop(n, step, 1)
@@ -210,7 +210,9 @@
 
     def spread(src, dst, size, at):
         mine = part(dst, me, size)
-        loop(n, lambda i: remote(src, mine, lax.rem(me + i, n), at), 1)
+        loop(n, lambda i: remote(
+            src, mine, lax.rem(me + lax.rem(i + n // 2 - 2, n - 1) + 1, n), at
+        ), 1)
         pltpu.make_async_copy(src, mine, rsem.at[at[1]]).start()
 
     def arrived(dst, at):

time: 66.1 us -> 67.6 us (1.023)
  Pallas kernels: 65.4 us -> 66.9 us
    pallas_call x1, Pallas kernels: 62.8 us -> 64.3 us  [shards(): pl.pallas_call(functools.partial(kernel, n, ntp, rows, width), out_shape=...]
where the time goes in v6:
time: 67.6 us; the launch traced here: 67.5 us
  Pallas kernels  66.9 us (99%)
    pallas_call x1, Pallas kernels, shards(): pl.pallas_call(functools.partial(kernel, n, ntp, rows, width), out_shape=...  64.3 us
    pallas_call x1, Pallas kernels, shards(): pl.pallas_call(deliver, out_shape=out_shape, in_specs=[anywhere] * 10, ou...  2.55 us

profile of v6, /device:TPU:1, one launch (start us, length us, event | category | flops | bytes accessed | tf_op | source)
XLA Modules:
  0.0 67.5 jit_solution(17081638869791186875)
XLA Ops:
  0.6 64.3 %shard_map.177 = (bf16[256,2048]{1,0:T(8,128)(2,1)S(1)}, bf16[256,2048]{1,0:T(8,128)(2,1)S(1)}, bf16[256,2048]{1,0:T(8,128)(2,1)S(1)}, bf16[256,2048]{1,0:T(8,12...) custom-call(bf16[256,2048]{1,0:T(8,128)(2,1)} %res_h.1, ...), custom_call_target="tpu_custom_call" | custom-call | tf_op jit(solution)/shard_map/pallas_call | solution.py:692
  65.0 2.5 %shard_map.178 = (bf16[256,2048]{1,0:T(8,128)(2,1)}, bf16[256,2048]{1,0:T(8,128)(2,1)}, bf16[256,2048]{1,0:T(8,128)(2,1)}, bf16[256,2048]{1,0:T(8,128)(2,1)}, bf...) custom-call(bf16[256,2048]{1,0:T(8,128)(2,1)S(1)} %get-tuple-element, ...), custom_call_target="tpu_custom_call" | custom-call | tf_op jit(solution)/shard_map/pallas_call | solution.py:705
